TPU v7x, 32 devices: a whole 2x2x4 slice. The times are simulated.
32 devices in a mesh: shard: 2 (over x), ctx: 4 (over y, core), tp: 4 (over z).
Axes of the slice: x: 2, y: 2, z: 4, core: 2. Of those that a mesh axis runs over, the one named last changes fastest.
Arguments:
- hidden_in: bfloat16 [4, 1024, 1024], P('shard', 'ctx'), may hold values from -6 to 6
- lengths: int32 [4], P('shard'), may hold values from 1 to 1024, as said below
- cotangent: bfloat16 [4, 1024, 1024], P('shard', 'ctx'), may hold values from -6 to 6
- ln1_gain: bfloat16 [1024], P(('shard', 'ctx')), may hold values from 0.5 to 1.5
- ln1_bias: bfloat16 [1024], P(('shard', 'ctx')), may hold values from -3 to 3
- w_qkv: bfloat16 [3, 1024, 1024], P(None, ('shard', 'ctx'), 'tp'), may hold values from -0.1875 to 0.1875
- b_qv: bfloat16 [2, 1024], P(None, 'tp'), may hold values from -3 to 3
- w_out: bfloat16 [1024, 1024], P(('shard', 'ctx'), 'tp'), may hold values from -1.5 to 1.5
- b_out: bfloat16 [1024], P(('shard', 'ctx')), may hold values from -3 to 3
- ln2_gain: bfloat16 [1024], P(('shard', 'ctx')), may hold values from 0.5 to 1.5
- ln2_bias: bfloat16 [1024], P(('shard', 'ctx')), may hold values from -3 to 3
- w_up: bfloat16 [1024, 4096], P(('shard', 'ctx'), 'tp'), may hold values from -0.1875 to 0.1875
- b_up: bfloat16 [4096], P('tp'), may hold values from -3 to 3
- w_down: bfloat16 [1024, 4096], P(('shard', 'ctx'), 'tp'), may hold values from -0.375 to 0.375
- b_down: bfloat16 [1024], P(('shard', 'ctx')), may hold values from -3 to 3
Outputs:
- hidden_out: float32 [4, 1024, 1024], P('shard', 'ctx')
- grad_in: float32 [4, 1024, 1024], P('shard', 'ctx')
- grad_ln1_gain: float32 [1024], P(('shard', 'ctx'))
- grad_ln1_bias: float32 [1024], P(('shard', 'ctx'))
- grad_w_qkv: float32 [3, 1024, 1024], P(None, ('shard', 'ctx'), 'tp')
- grad_b_qv: float32 [2, 1024], P(None, 'tp')
- grad_w_out: float32 [1024, 1024], P(('shard', 'ctx'), 'tp')
- grad_b_out: float32 [1024], P(('shard', 'ctx'))
- grad_ln2_gain: float32 [1024], P(('shard', 'ctx'))
- grad_ln2_bias: float32 [1024], P(('shard', 'ctx'))
- grad_w_up: float32 [1024, 4096], P(('shard', 'ctx'), 'tp')
- grad_b_up: float32 [4096], P('tp')
- grad_w_down: float32 [1024, 4096], P(('shard', 'ctx'), 'tp')
- grad_b_down: float32 [1024], P(('shard', 'ctx'))
Inputs may be any that keep to these rules, and one draw needn't show every extreme that they name: Sequence i belongs to shard group i // 2; its positions from lengths[i] on are padding. Some sequence has all 1024 positions live.
All inputs are finite; a program needn't handle non-finite values.
Results may differ from a plain program's by a relative error of at most 0.012.
The roundings to bfloat16 on the way count: a program that leaves them out, or rounds other values in their place, can miss the bound.
Values may be sent and summed in bfloat16 or wider, within the bound.
A program may use at most 128 MiB of HBM per device.

v0:
```python
import math

import jax
import jax.numpy as jnp
from jax import lax
from jax.sharding import PartitionSpec as P

HD = 64


EPS = 1e-05
KAPPA = math.sqrt(2.0 / math.pi)


def normalize(row, gain, shift):
    center = jnp.mean(row, axis=-1, keepdims=True)
    centred = row - center
    inv_std = lax.rsqrt(jnp.mean(centred * centred, axis=-1, keepdims=True) + EPS)
    unit_rows = centred * inv_std
    return (unit_rows * gain + shift, unit_rows, inv_std)


def normalize_back(grad_out, unit_rows, inv_std, gain):
    scaled = grad_out * gain
    return inv_std * (
        scaled
        - jnp.mean(scaled, axis=-1, keepdims=True)
        - unit_rows * jnp.mean(scaled * unit_rows, axis=-1, keepdims=True)
    )


def gelu_pair(pre_act):
    inner = KAPPA * (pre_act + 0.044715 * pre_act * pre_act * pre_act)
    tanh_val = jnp.tanh(inner)
    value_out = 0.5 * pre_act * (1.0 + tanh_val)
    slope = 0.5 * (1.0 + tanh_val) + 0.5 * pre_act * (1.0 - tanh_val * tanh_val) * KAPPA * (
        1.0 + 3.0 * 0.044715 * pre_act * pre_act
    )
    return (value_out, slope)


def contract_last(left, right):
    return lax.dot_general(
        left, right, (((1,), (1,)), ((), ())), preferred_element_type=jnp.float32
    )


def contract_first(left, right):
    return lax.dot_general(
        left, right, (((0,), (0,)), ((), ())), preferred_element_type=jnp.float32
    )


def on_device(
    hidden_in,
    lengths,
    cotangent,
    ln1_gain,
    ln1_bias,
    w_qkv,
    b_qv,
    w_out,
    b_out,
    ln2_gain,
    ln2_bias,
    w_up,
    b_up,
    w_down,
    b_down,
):
    groups, block_len, width = hidden_in.shape
    head_width = w_qkv.shape[2]
    heads_here = head_width // HD
    row_count = groups * block_len
    scale = 1.0 / math.sqrt(HD)
    vectors = jnp.stack([ln1_gain, ln1_bias, b_out, ln2_gain, ln2_bias, b_down], 0)
    fetched = (
        lax.all_gather(w_qkv, ("shard", "ctx"), axis=1, tiled=True),
        lax.all_gather(w_out, ("shard", "ctx"), axis=0, tiled=True),
        lax.all_gather(w_up, ("shard", "ctx"), axis=0, tiled=True),
        lax.all_gather(w_down, ("shard", "ctx"), axis=0, tiled=True),
        lax.all_gather(vectors, ("shard", "ctx"), axis=1, tiled=True),
    )
    qkv_full, out_full, up_full, down_full, vec_full = fetched
    vec_wide = vec_full.astype(jnp.float32)
    gain_one = vec_wide[0]
    shift_one = vec_wide[1]
    bias_out = vec_wide[2]
    gain_two = vec_wide[3]
    shift_two = vec_wide[4]
    bias_down = vec_wide[5]
    ctx_index = lax.axis_index("ctx")
    positions = jnp.arange(block_len, dtype=jnp.int32) + ctx_index * block_len
    live_rows = (positions[None, :] < lengths[:, None]).reshape(row_count, 1)

    def allowed_mask(start, count):
        key_pos = start + jnp.arange(count, dtype=jnp.int32)
        causal = key_pos[None, None, None, :] <= positions[None, None, :, None]
        inside = key_pos[None, None, None, :] < lengths[:, None, None, None]
        return causal & inside

    inputs = hidden_in.reshape(row_count, width).astype(jnp.float32)
    normed_one, unit_one, inv_one = normalize(inputs, gain_one, shift_one)
    normed_bf = normed_one.astype(jnp.bfloat16)
    projected = jnp.einsum("rd,jde->jre", normed_bf, qkv_full, preferred_element_type=jnp.float32)
    query = (projected[0] + b_qv[0].astype(jnp.float32)).astype(jnp.bfloat16)
    keys_here = projected[1].astype(jnp.bfloat16).reshape(groups, block_len, head_width)
    values_here = (
        (projected[2] + b_qv[1].astype(jnp.float32))
        .astype(jnp.bfloat16)
        .reshape(groups, block_len, head_width)
    )
    query_heads = query.reshape(groups, block_len, heads_here, HD)

    def fold_keys(step_fn, init):
        return step_fn(
            init,
            (
                lax.all_gather(keys_here, "ctx", axis=1, tiled=True),
                lax.all_gather(values_here, "ctx", axis=1, tiled=True),
            ),
            jnp.int32(0),
        )

    def piece_scores(piece, start):
        key_piece, value_piece = piece
        count = key_piece.shape[1]
        key_heads = key_piece.reshape(groups, count, heads_here, HD)
        value_heads = value_piece.reshape(groups, count, heads_here, HD)
        scores = (
            jnp.einsum(
                "sqhd,skhd->shqk", query_heads, key_heads, preferred_element_type=jnp.float32
            )
            * scale
        )
        allowed = allowed_mask(start, count)
        return (jnp.where(allowed, scores, -1e30), allowed, value_heads)

    def totals_step(carry, piece, start):
        top, total = carry
        scores, allowed, unused = piece_scores(piece, start)
        new_top = jnp.maximum(top, jnp.max(scores, axis=-1))
        weights = jnp.where(allowed, jnp.exp(scores - new_top[..., None]), 0.0)
        total = jnp.sum(weights, axis=-1)
        return (new_top, total)

    start_totals = (
        jnp.full((groups, heads_here, block_len), -1e30, jnp.float32),
        jnp.zeros((groups, heads_here, block_len), jnp.float32),
    )
    top, total = fold_keys(totals_step, start_totals)
    log_total = top + jnp.log(total)

    def values_step(accum, piece, start):
        scores, allowed, value_heads = piece_scores(piece, start)
        probs_piece = jnp.where(allowed, jnp.exp(scores - log_total[..., None]), 0.0).astype(
            jnp.bfloat16
        )
        return jnp.einsum(
            "shqk,skhd->sqhd", probs_piece, value_heads, preferred_element_type=jnp.float32
        )

    accum = fold_keys(values_step, jnp.zeros((groups, block_len, heads_here, HD), jnp.float32))
    attended_heads = accum.astype(jnp.bfloat16)
    attended = attended_heads.reshape(row_count, head_width)
    proj_sum = lax.psum(contract_last(attended, out_full), "tp")
    resid = inputs + proj_sum + bias_out
    normed_two, unit_two, inv_two = normalize(resid, gain_two, shift_two)
    second_bf = normed_two.astype(jnp.bfloat16)
    pre_act = jnp.dot(second_bf, up_full, preferred_element_type=jnp.float32) + b_up.astype(
        jnp.float32
    )
    activ, slope = gelu_pair(pre_act)
    hidden = activ.astype(jnp.bfloat16)
    mlp_sum = lax.psum(contract_last(hidden, down_full), "tp")
    result = jnp.where(live_rows, resid + mlp_sum + bias_down, 0.0)
    again = (
        lax.all_gather(w_qkv, ("shard", "ctx"), axis=1, tiled=True),
        lax.all_gather(w_out, ("shard", "ctx"), axis=0, tiled=True),
        lax.all_gather(w_up, ("shard", "ctx"), axis=0, tiled=True),
        lax.all_gather(w_down, ("shard", "ctx"), axis=0, tiled=True),
    )
    qkv_back, out_back, up_back, down_back = again
    grad_rows = jnp.where(live_rows, cotangent.reshape(row_count, width).astype(jnp.float32), 0.0)
    grad_bf = grad_rows.astype(jnp.bfloat16)
    grad_bias_down = jnp.sum(grad_rows, axis=0)
    grad_down = contract_first(grad_bf, hidden)
    d_pre = jnp.dot(grad_bf, down_back, preferred_element_type=jnp.float32) * slope
    d_pre_bf = d_pre.astype(jnp.bfloat16)
    grad_bias_up = jnp.sum(d_pre, axis=0)
    grad_up = contract_first(second_bf, d_pre_bf)
    back_two = lax.psum(contract_last(d_pre_bf, up_back), "tp")
    grad_gain_two = jnp.sum(back_two * unit_two, axis=0)
    grad_shift_two = jnp.sum(back_two, axis=0)
    d_resid = grad_rows + normalize_back(back_two, unit_two, inv_two, gain_two)
    d_resid_bf = d_resid.astype(jnp.bfloat16)
    grad_bias_out = jnp.sum(d_resid, axis=0)
    grad_out = contract_first(d_resid_bf, attended)
    d_attended = jnp.dot(d_resid_bf, out_back, preferred_element_type=jnp.float32).astype(
        jnp.bfloat16
    )
    keys_whole, values_whole = (
        lax.all_gather(keys_here, "ctx", axis=1, tiled=True),
        lax.all_gather(values_here, "ctx", axis=1, tiled=True),
    )
    seq_len = keys_whole.shape[1]
    key_heads = keys_whole.reshape(groups, seq_len, heads_here, HD)
    value_heads = values_whole.reshape(groups, seq_len, heads_here, HD)
    scores = (
        jnp.einsum("sqhd,skhd->shqk", query_heads, key_heads, preferred_element_type=jnp.float32)
        * scale
    )
    allowed = allowed_mask(0, seq_len)
    exact_probs = jnp.where(allowed, jnp.exp(scores - log_total[..., None]), 0.0)
    d_att_heads = d_attended.reshape(groups, block_len, heads_here, HD)
    delta = jnp.transpose(
        jnp.sum(d_att_heads.astype(jnp.float32) * attended_heads.astype(jnp.float32), axis=-1),
        (0, 2, 1),
    )
    d_probs = jnp.einsum(
        "sqhd,skhd->shqk", d_att_heads, value_heads, preferred_element_type=jnp.float32
    )
    d_scores = (exact_probs * (d_probs - delta[..., None])).astype(jnp.bfloat16)
    d_query = (
        jnp.einsum("shqk,skhd->sqhd", d_scores, key_heads, preferred_element_type=jnp.float32)
        * scale
    )
    probs_bf = exact_probs.astype(jnp.bfloat16)
    key_terms = (
        jnp.einsum("shqk,sqhd->skhd", d_scores, query_heads, preferred_element_type=jnp.float32)
        * scale
    )
    value_terms = jnp.einsum(
        "shqk,sqhd->skhd", probs_bf, d_att_heads, preferred_element_type=jnp.float32
    )
    d_keys, d_values = (
        lax.psum_scatter(
            key_terms.reshape(groups, seq_len, head_width), "ctx", scatter_dimension=1, tiled=True
        ),
        lax.psum_scatter(
            value_terms.reshape(groups, seq_len, head_width), "ctx", scatter_dimension=1, tiled=True
        ),
    )
    d_query_rows = d_query.reshape(row_count, head_width)
    d_value_rows = d_values.reshape(row_count, head_width)
    grad_bias_qv = jnp.stack([jnp.sum(d_query_rows, axis=0), jnp.sum(d_value_rows, axis=0)], 0)
    stacked = jnp.stack(
        [d_query_rows, d_keys.reshape(row_count, head_width), d_value_rows], 0
    ).astype(jnp.bfloat16)
    grad_qkv = jnp.einsum("rd,jre->jde", normed_bf, stacked, preferred_element_type=jnp.float32)
    back_one = lax.psum(
        jnp.einsum("jre,jde->rd", stacked, qkv_back, preferred_element_type=jnp.float32), "tp"
    )
    grad_gain_one = jnp.sum(back_one * unit_one, axis=0)
    grad_shift_one = jnp.sum(back_one, axis=0)
    d_inputs = d_resid + normalize_back(back_one, unit_one, inv_one, gain_one)
    vec_grads = jnp.stack(
        [
            grad_gain_one,
            grad_shift_one,
            grad_bias_out,
            grad_gain_two,
            grad_shift_two,
            grad_bias_down,
        ],
        0,
    )
    summed = (
        lax.psum_scatter(grad_qkv, ("shard", "ctx"), scatter_dimension=1, tiled=True),
        lax.psum_scatter(grad_out, ("shard", "ctx"), scatter_dimension=0, tiled=True),
        lax.psum_scatter(grad_up, ("shard", "ctx"), scatter_dimension=0, tiled=True),
        lax.psum_scatter(grad_down, ("shard", "ctx"), scatter_dimension=0, tiled=True),
        lax.psum_scatter(vec_grads, ("shard", "ctx"), scatter_dimension=1, tiled=True),
    )
    sum_qkv, sum_out, sum_up, sum_down, sum_vec = summed
    bias_qv_sum, bias_up_sum = lax.psum((grad_bias_qv, grad_bias_up), ("shard", "ctx"))
    return (
        result.reshape(groups, block_len, width),
        d_inputs.reshape(groups, block_len, width),
        sum_vec[0],
        sum_vec[1],
        sum_qkv,
        bias_qv_sum,
        sum_out,
        sum_vec[2],
        sum_vec[3],
        sum_vec[4],
        sum_up,
        bias_up_sum,
        sum_down,
        sum_vec[5],
    )


def solution(mesh):
    return jax.shard_map(
        on_device,
        mesh=mesh,
        in_specs=(
            P("shard", "ctx", None),
            P("shard"),
            P("shard", "ctx", None),
            P(("shard", "ctx")),
            P(("shard", "ctx")),
            P(None, ("shard", "ctx"), "tp"),
            P(None, "tp"),
            P(("shard", "ctx"), "tp"),
            P(("shard", "ctx")),
            P(("shard", "ctx")),
            P(("shard", "ctx")),
            P(("shard", "ctx"), "tp"),
            P("tp"),
            P(("shard", "ctx"), "tp"),
            P(("shard", "ctx")),
        ),
        out_specs=(
            P("shard", "ctx", None),
            P("shard", "ctx", None),
            P(("shard", "ctx")),
            P(("shard", "ctx")),
            P(None, ("shard", "ctx"), "tp"),
            P(None, "tp"),
            P(("shard", "ctx"), "tp"),
            P(("shard", "ctx")),
            P(("shard", "ctx")),
            P(("shard", "ctx")),
            P(("shard", "ctx"), "tp"),
            P("tp"),
            P(("shard", "ctx"), "tp"),
            P(("shard", "ctx")),
        ),
        check_vma=False,
    )
```

profile of v0, /device:TPU:0, one launch (start us, length us, event | category | flops | bytes accessed | tf_op | source)
XLA Modules:
  0.0 817.6 jit_solution(358480449158023805)
XLA Ops:
  8.0 1.4 convert_reduce_fusion
  9.5 1.6 fusion.14
  11.3 10.3 %all_gather.28 = bf16[6,1024]{1,0:T(8,128)(2,1)S(1)} all-gather(bf16[6,128]{1,0:T(8,128)(2,1)S(1)} %stack.61), channel_id=1, replica_groups=mesh['shard'=2,'ctx'=4,'tp'=4] {'shard','ctx'}, dimensions={1}, use_global_device_ids=true | all-gather | bytes 13824 | tf_op jit(solution)/shard_map/all_gather | solution.py:82
  21.7 1.4 fusion.21
  23.1 15.3 %all-gather.6.cloned.1.call-done = bf16[3,1024,256]{2,1,0:T(8,128)(2,1)} async-done(((bf16[3,128,256]{2,1,0:T(8,128)(2,1)}), bf16[3,1024,256]{2,1,0:T(8,128)(2,1)}) %all-gather.6.cloned.1.call-update) | async-done | bytes 1572880 | tf_op jit(solution)/shard_map/all_gather | solution.py:78
  38.4 2.7 convolution_bitcast_fusion.2
  41.2 0.8 slice.87
  42.1 10.8 %all_gather.32 = bf16[1024,256]{1,0:T(8,128)(2,1)} all-gather(bf16[128,256]{1,0:T(8,128)(2,1)S(1)} %copy-done.20), channel_id=1, replica_groups=mesh['shard'=2,'ctx'=4,'tp'=4] {'shard','ctx'}, dimensions={0}, use_global_device_ids=true | all-gather | bytes 589824 | tf_op jit(solution)/shard_map/all_gather | solution.py:79
  53.5 2.3 fusion.56
  56.5 2.0 add_convert_fusion.2
  58.8 1.5 copy.55
  60.3 1.8 fusion
  62.2 3.0 select_reduce_fusion
  65.4 12.3 %all-gather.8.cloned.1.call-done = bf16[2,1024,256]{2,1,0:T(8,128)(2,1)} async-done(((bf16[2,256,256]{2,1,0:T(8,128)(2,1)}), bf16[2,1024,256]{2,1,0:T(8,128)(2,1)}) %all-gather.8.cloned.1.call-update) | async-done | bytes 1048592 | tf_op jit(solution)/shard_map/all_gather | solution.py:120
  77.7 1.5 copy.52
  79.3 6.0 fusion.31
  86.0 1.8 fusion.61
  89.3 1.2 fusion.28
  90.5 83.9 %all-reduce.6.cloned.1.call-done = f32[512,1024]{1,0:T(8,128)} async-done(((f32[512,1024]{1,0:T(8,128)}), f32[512,1024]{1,0:T(8,128)}) %all-reduce.6.cloned.1.call-update) | async-done | bytes 2097168 | tf_op jit(solution)/shard_map/psum | solution.py:166
  174.5 1.9 fusion.54
  176.8 26.5 %all-gather.12.cloned.1.call-done = bf16[1024,1024]{1,0:T(8,128)(2,1)} async-done(((bf16[128,1024]{1,0:T(8,128)(2,1)}), bf16[1024,1024]{1,0:T(8,128)(2,1)}) %all-gather.12.cloned.1.call-update) | async-done | bytes 2097168 | tf_op jit(solution)/shard_map/all_gather | solution.py:80
  203.3 4.2 fusion.52
  207.5 25.6 %all-gather.14.cloned.1.call-done = bf16[1024,1024]{1,0:T(8,128)(2,1)} async-done(((bf16[128,1024]{1,0:T(8,128)(2,1)}), bf16[1024,1024]{1,0:T(8,128)(2,1)}) %all-gather.14.cloned.1.call-update) | async-done | bytes 2097168 | tf_op jit(solution)/shard_map/all_gather | solution.py:81
  233.1 5.0 fusion.60
  238.1 1.1 copy-done.31
  239.2 2.6 fusion.39
  241.9 86.6 %all-reduce.8.cloned.1.call-done = f32[512,1024]{1,0:T(8,128)} async-done(((f32[512,1024]{1,0:T(8,128)}), f32[512,1024]{1,0:T(8,128)}) %all-reduce.8.cloned.1.call-update) | async-done | bytes 2097168 | tf_op jit(solution)/shard_map/psum | solution.py:192
  328.5 2.6 multiply_reduce_fusion
  331.1 1.1 fusion.53
  332.2 1.4 copy-done.2
  333.6 1.1 convolution_convert_fusion
  334.7 2.0 reshape.250
  336.8 2.0 copy.58
  338.7 1.1 multiply_reduce_fusion.5
  339.8 6.1 multiply_convert_fusion
  346.0 2.6 convolution_multiply_fusion
  348.7 6.8 fusion.2
  355.8 5.3 fusion.51
  361.1 2.1 fusion.57
  363.2 2.0 copy.70
  365.2 2.2 reshape.249
  367.3 11.8 %reduce-scatter.8.cloned.1.call-done = f32[2,256,256]{1,2,0:T(8,128)} async-done(((f32[2,1024,256]{1,2,0:T(8,128)}), f32[2,256,256]{1,2,0:T(8,128)}) %reduce-scatter.8.cloned.1.call-update) | async-done | bytes 524304 | tf_op jit(solution)/shard_map/reduce_scatter | solution.py:237
  379.2 1.8 convert.21
  380.9 1.8 copy.61
  382.7 30.6 %reduce-scatter.10.cloned.1.call-done = f32[2,256,256]{1,2,0:T(8,128)} async-done(((f32[2,1024,256]{1,2,0:T(8,128)}), f32[2,256,256]{1,2,0:T(8,128)}) %reduce-scatter.10.cloned.1.call-update) | async-done | bytes 524304 | tf_op jit(solution)/shard_map/reduce_scatter | solution.py:240
  413.4 2.0 fusion.58
  415.3 1.8 copy.63
  417.1 4.0 convolution_bitcast_fusion.1
  421.2 1.5 select_reduce_fusion.1
  422.7 153.9 %all-reduce.10.cloned.1.call-done = (f32[512,1024]{1,0:T(8,128)}, f32[512,1024]{1,0:T(8,128)}) async-done(((f32[512,1024]{1,0:T(8,128)}, f32[512,1024]{1,0:T(8,128)}), (f32[512,1024]{1,0:T(8,128)}, f32[512,1024]{1,0:T(8,128)})) %all-reduce.10.cloned.1.call-update) | async-done | bytes 4194320 | tf_op jit(solution)/shard_map/psum | solution.py:175
  576.7 2.5 fusion.26
  579.9 4.3 convolution_bitcast_fusion
  584.2 3.1 fusion.34
  587.4 5.3 fusion.50
  592.7 4.6 fusion.37
  597.5 14.4 %all-reduce = (f32[2,256]{1,0:T(2,128)}, f32[1024]{0:T(1024)}) all-reduce(f32[2,256]{1,0:T(2,128)S(1)} %pad_maximum_fusion.3, f32[1024]{0:T(1024)S(1)} %get-tuple-element.95), channel_id=1, replica_groups=mesh['shard'=2,'ctx'=4,'tp'=4] {'shard','ctx'}, use_global_device_ids=true, to_apply=%region_27.28 | all-reduce | flops 1536 | bytes 12288 | tf_op jit(solution)/shard_map/psum | solution.py:276
  611.9 3.3 add_select_fusion
  615.3 2.0 fusion.25
  617.3 1.4 slice_bitcast_fusion
  618.7 41.6 %reduce-scatter.14.cloned.1.call-done = f32[3,128,256]{1,2,0:T(8,128)} async-done(((f32[3,1024,256]{1,2,0:T(8,128)}), f32[3,128,256]{1,2,0:T(8,128)}) %reduce-scatter.14.cloned.1.call-update) | async-done | bytes 393232 | tf_op jit(solution)/shard_map/reduce_scatter | solution.py:269
  660.3 1.9 copy.66
  662.2 38.2 %reduce-scatter.16.cloned.1.call-done = f32[128,256]{1,0:T(8,128)} async-done(((f32[1024,256]{1,0:T(8,128)}), f32[128,256]{1,0:T(8,128)}) %reduce-scatter.16.cloned.1.call-update) | async-done | bytes 131088 | tf_op jit(solution)/shard_map/reduce_scatter | solution.py:270
  700.4 55.5 %reduce-scatter.20.cloned.1.call-done = f32[128,1024]{1,0:T(8,128)} async-done(((f32[1024,1024]{1,0:T(8,128)}), f32[128,1024]{1,0:T(8,128)}) %reduce-scatter.20.cloned.1.call-update) | async-done | bytes 524304 | tf_op jit(solution)/shard_map/reduce_scatter | solution.py:272
  755.9 55.1 %reduce-scatter.18.cloned.1.call-done = f32[128,1024]{1,0:T(8,128)} async-done(((f32[1024,1024]{1,0:T(8,128)}), f32[128,1024]{1,0:T(8,128)}) %reduce-scatter.18.cloned.1.call-update) | async-done | bytes 524304 | tf_op jit(solution)/shard_map/reduce_scatter | solution.py:271
  (125 shorter events, 7.0 us)
Async XLA Ops:
  7.2 14.5 %copy-start = (bf16[2,256,1024]{2,1,0:T(8,128)(2,1)S(1)}, bf16[2,256,1024]{2,1,0:T(8,128)(2,1)}, u32[]{:S(2)}) copy-start(bf16[2,256,1024]{2,1,0:T(8,128)(2,1)} %param.15) | copy-start | bytes 3145732
  7.2 4.0 copy-start.29
  7.2 4.0 copy-start.28
  7.2 4.0 copy-start.27
  7.2 4.0 copy-start.26
  7.2 4.0 copy-start.25
  7.2 4.0 copy-start.24
  7.3 14.4 %copy-start.21 = (bf16[2,256]{1,0:T(2,128)(2,1)S(1)}, bf16[2,256]{1,0:T(2,128)(2,1)}, u32[]{:S(2)}) copy-start(bf16[2,256]{1,0:T(2,128)(2,1)} %param.21) | copy-start | bytes 3076
  7.3 31.2 %all-gather.6.cloned.1.call-start = ((), (), s32[]{:S(2)}) async-start(), calls=%async_computation.7 | async-start | bytes 1769472 | tf_op jit(solution)/shard_map/all_gather | solution.py:78
  8.0 50.8 %all-gather.10.cloned.1.call-start = ((), (), s32[]{:S(2)}) async-start(), calls=%async_computation.9 | async-start | bytes 1310720 | tf_op jit(solution)/shard_map/all_gather | solution.py:119
  23.1 19.0 %copy-start.20 = (bf16[128,256]{1,0:T(8,128)(2,1)S(1)}, bf16[128,256]{1,0:T(8,128)(2,1)}, u32[]{:S(2)}) copy-start(bf16[128,256]{1,0:T(8,128)(2,1)} %param.22) | copy-start | bytes 196612
  23.1 29.8 %copy-start.23 = (s32[2]{0:T(128)S(1)}, s32[2]{0:T(128)}, u32[]{:S(2)}) copy-start(s32[2]{0:T(128)} %param.16) | copy-start | bytes 28
  41.1 12.0 %copy-start.17 = (f32[3,512,256]{2,1,0:T(8,128)}, f32[3,512,256]{2,1,0:T(8,128)S(1)}, u32[]{:S(2)}) copy-start(f32[3,512,256]{2,1,0:T(8,128)S(1)} %convolution_bitcast_fusion.2) | copy-start | bytes 4718596
  42.0 35.8 %all-gather.8.cloned.1.call-start = ((), (), s32[]{:S(2)}) async-start(), calls=%async_computation.8 | async-start | bytes 1310720 | tf_op jit(solution)/shard_map/all_gather | solution.py:120
  53.4 25.8 %copy-start.14 = (pred[2,256,1024]{2,1,0:T(8,128)(4,1)}, pred[2,256,1024]{2,1,0:T(8,128)(4,1)S(1)}, u32[]{:S(2)}) copy-start(pred[2,256,1024]{2,1,0:T(8,128)(4,1)S(1)} %broadcast_and_fusion) | copy-start | bytes 1572868
  56.5 5.7 copy-start.12
  58.5 116.0 %all-reduce.6.cloned.1.call-start = ((), (), s32[]{:S(2)}) async-start(), calls=%async_computation.10 | async-start | bytes 4194304 | tf_op jit(solution)/shard_map/psum | solution.py:166
  60.3 1.9 copy-start.8
  62.2 3.2 copy-start.1
  79.2 6.0 copy-start.18
  79.3 6.7 copy-start.15
  85.3 0.7 copy-start.19
  86.0 3.3 copy-start.22
  86.0 3.3 copy-start.6
  87.8 115.4 %all-gather.12.cloned.1.call-start = ((), (), s32[]{:S(2)}) async-start(), calls=%async_computation.11 | async-start | bytes 2359296 | tf_op jit(solution)/shard_map/all_gather | solution.py:80
  88.4 144.7 %all-gather.14.cloned.1.call-start = ((), (), s32[]{:S(2)}) async-start(), calls=%async_computation.12 | async-start | bytes 2359296 | tf_op jit(solution)/shard_map/all_gather | solution.py:81
  89.0 239.5 %all-reduce.8.cloned.1.call-start = ((), (), s32[]{:S(2)}) async-start(), calls=%async_computation.13 | async-start | bytes 4194304 | tf_op jit(solution)/shard_map/psum | solution.py:192
  233.1 6.1 copy-start.30
  238.1 1.1 copy-start.31
  241.8 137.4 %reduce-scatter.8.cloned.1.call-start = ((), (), s32[]{:S(2)}) async-start(), calls=%async_computation.14 | async-start | bytes 2621440 | tf_op jit(solution)/shard_map/reduce_scatter | solution.py:237
  328.5 2.6 copy-start.7
  328.5 2.6 copy-start.10
  331.1 2.5 copy-start.16
  332.2 1.4 copy-start.2
  339.8 6.1 copy-start.13
  346.0 2.7 copy-start.4
  348.6 64.7 %reduce-scatter.10.cloned.1.call-start = ((), (), s32[]{:S(2)}) async-start(), calls=%async_computation.15 | async-start | bytes 2621440 | tf_op jit(solution)/shard_map/reduce_scatter | solution.py:240
  355.5 221.2 %all-reduce.10.cloned.1.call-start = ((), (), s32[]{:S(2)}) async-start(), calls=%async_computation.21 | async-start | bytes 8388608 | tf_op jit(solution)/shard_map/psum | solution.py:175
  355.7 5.4 copy-start.5
  355.7 5.3 copy-start.9
  421.2 196.1 %reduce-scatter.12.cloned.1.call-start = ((), (), s32[]{:S(2)}) async-start(), calls=%async_computation.16 | async-start | bytes 36864 | tf_op jit(solution)/shard_map/reduce_scatter | solution.py:273
  579.9 80.5 %reduce-scatter.14.cloned.1.call-start = ((), (), s32[]{:S(2)}) async-start(), calls=%async_computation.17 | async-start | bytes 3538944 | tf_op jit(solution)/shard_map/reduce_scatter | solution.py:269
  584.2 116.3 %reduce-scatter.16.cloned.1.call-start = ((), (), s32[]{:S(2)}) async-start(), calls=%async_computation.18 | async-start | bytes 1179648 | tf_op jit(solution)/shard_map/reduce_scatter | solution.py:270
  587.3 168.6 %reduce-scatter.20.cloned.1.call-start = ((), (), s32[]{:S(2)}) async-start(), calls=%async_computation.20 | async-start | bytes 4718592 | tf_op jit(solution)/shard_map/reduce_scatter | solution.py:272
  592.7 218.4 %reduce-scatter.18.cloned.1.call-start = ((), (), s32[]{:S(2)}) async-start(), calls=%async_computation.19 | async-start | bytes 4718592 | tf_op jit(solution)/shard_map/reduce_scatter | solution.py:271
  611.9 3.3 copy-start.3
  611.9 3.3 copy-start.11
Sparse Core Ops, SparseCore 0:
  10.0 28.3 all-gather.5
  42.1 16.7 all-gather.9
  61.0 16.7 all-gather.7
  87.9 86.4 all-reduce.5
  176.4 26.8 all-gather.11
  205.2 27.8 all-gather.13
  241.9 86.5 all-reduce.7
  348.8 30.3 reduce-scatter.7
  381.9 31.4 reduce-scatter.9
  421.3 155.3 all-reduce.9
  580.5 30.2 reduce-scatter.11
  614.0 46.2 reduce-scatter.13
  664.4 36.0 reduce-scatter.15
  704.6 51.2 reduce-scatter.19
  759.7 51.3 reduce-scatter.17
where the time goes:
time: 819 us; the launch traced here: 818 us
  waiting for transfers between devices  639 us (78%)
  matrix products  69.5 us (8%)
  blocking collectives  35.5 us (4%)
  other arithmetic  31.6 us (4%)
  local copies, waits for them, and re-layouts  26.2 us (3%)
  between operations  14.5 us (2%)
    psum x1, waiting for transfers between devices, on_device(): mlp_sum = lax.psum(contract_last(hidden, down_full), 'tp')  154 us
    psum x1, waiting for transfers between devices, on_device(): back_two = lax.psum(contract_last(d_pre_bf, up_back), 'tp')  86.6 us
    psum x1, waiting for transfers between devices, on_device(): proj_sum = lax.psum(contract_last(attended, out_full), 'tp')  83.9 us
    reduce_scatter x1, waiting for transfers between devices, on_device(): lax.psum_scatter(grad_down, ('shard', 'ctx'), scatter_dimension=0, tiled=...  55.5 us
    reduce_scatter x1, waiting for transfers between devices, on_device(): lax.psum_scatter(grad_up, ('shard', 'ctx'), scatter_dimension=0, tiled=True)  55.1 us
    reduce_scatter x1, waiting for transfers between devices, on_device(): lax.psum_scatter(grad_qkv, ('shard', 'ctx'), scatter_dimension=1, tiled=T...  41.6 us
    reduce_scatter x1, waiting for transfers between devices, on_device(): lax.psum_scatter(grad_out, ('shard', 'ctx'), scatter_dimension=0, tiled=T...  38.2 us
    reduce_scatter x1, waiting for transfers between devices, on_device(): lax.psum_scatter(value_terms.reshape(groups, seq_len, head_width), 'ctx',...  30.6 us
  transfers between devices with their start and end apart: 15, of which 14 were waited for; matrix products, arithmetic and copies ran while one was open for 9% of the time, Pallas kernels for 0%

commit v1 on v0

--- a/solution.py
+++ b/solution.py
@@ -49,6 +49,10 @@
     return lax.dot_general(
         left, right, (((0,), (0,)), ((), ())), preferred_element_type=jnp.float32
     )
+
+
+def sum_tp(part):
+    return lax.psum(part.astype(jnp.bfloat16), "tp").astype(jnp.float32)
 
 
 def on_device(
@@ -73,16 +77,20 @@
     heads_here = head_width // HD
     row_count = groups * block_len
     scale = 1.0 / math.sqrt(HD)
-    vectors = jnp.stack([ln1_gain, ln1_bias, b_out, ln2_gain, ln2_bias, b_down], 0)
-    fetched = (
-        lax.all_gather(w_qkv, ("shard", "ctx"), axis=1, tiled=True),
-        lax.all_gather(w_out, ("shard", "ctx"), axis=0, tiled=True),
-        lax.all_gather(w_up, ("shard", "ctx"), axis=0, tiled=True),
-        lax.all_gather(w_down, ("shard", "ctx"), axis=0, tiled=True),
-        lax.all_gather(vectors, ("shard", "ctx"), axis=1, tiled=True),
-    )
-    qkv_full, out_full, up_full, down_full, vec_full = fetched
-    vec_wide = vec_full.astype(jnp.float32)
+    rows_own = w_out.shape[0]
+    vectors = jnp.stack([ln1_gain, ln1_bias, b_out, ln2_gain, ln2_bias, b_down], 1)
+    packed_one = jnp.concatenate(
+        [w_qkv[0], w_qkv[1], w_qkv[2], w_out, jnp.pad(vectors, ((0, 0), (0, 122)))], 1
+    )
+    packed_two = jnp.concatenate([w_up, w_down], 1)
+    whole_one = lax.all_gather(packed_one, ("shard", "ctx"), axis=0, tiled=True)
+    whole_two = lax.all_gather(packed_two, ("shard", "ctx"), axis=0, tiled=True)
+    qkv_width = 3 * head_width
+    qkv_full = whole_one[:, :qkv_width]
+    out_full = whole_one[:, qkv_width : qkv_width + head_width]
+    vec_wide = whole_one[:, qkv_width + head_width :].astype(jnp.float32).T
+    up_full = whole_two[:, : w_up.shape[1]]
+    down_full = whole_two[:, w_up.shape[1] :]
     gain_one = vec_wide[0]
     shift_one = vec_wide[1]
     bias_out = vec_wide[2]
@@ -102,7 +110,8 @@
     inputs = hidden_in.reshape(row_count, width).astype(jnp.float32)
     normed_one, unit_one, inv_one = normalize(inputs, gain_one, shift_one)
     normed_bf = normed_one.astype(jnp.bfloat16)
-    projected = jnp.einsum("rd,jde->jre", normed_bf, qkv_full, preferred_element_type=jnp.float32)
+    product = jnp.dot(normed_bf, qkv_full, preferred_element_type=jnp.float32)
+    projected = [product[:, j * head_width : (j + 1) * head_width] for j in range(3)]
     query = (projected[0] + b_qv[0].astype(jnp.float32)).astype(jnp.bfloat16)
     keys_here = projected[1].astype(jnp.bfloat16).reshape(groups, block_len, head_width)
     values_here = (
@@ -112,15 +121,13 @@
     )
     query_heads = query.reshape(groups, block_len, heads_here, HD)
 
+    kv_whole = lax.all_gather(
+        jnp.concatenate([keys_here, values_here], -1), "ctx", axis=1, tiled=True
+    )
+    keys_whole, values_whole = kv_whole[..., :head_width], kv_whole[..., head_width:]
+
     def fold_keys(step_fn, init):
-        return step_fn(
-            init,
-            (
-                lax.all_gather(keys_here, "ctx", axis=1, tiled=True),
-                lax.all_gather(values_here, "ctx", axis=1, tiled=True),
-            ),
-            jnp.int32(0),
-        )
+        return step_fn(init, (keys_whole, values_whole), jnp.int32(0))
 
     def piece_scores(piece, start):
         key_piece, value_piece = piece
@@ -163,7 +170,7 @@
     accum = fold_keys(values_step, jnp.zeros((groups, block_len, heads_here, HD), jnp.float32))
     attended_heads = accum.astype(jnp.bfloat16)
     attended = attended_heads.reshape(row_count, head_width)
-    proj_sum = lax.psum(contract_last(attended, out_full), "tp")
+    proj_sum = sum_tp(contract_last(attended, out_full))
     resid = inputs + proj_sum + bias_out
     normed_two, unit_two, inv_two = normalize(resid, gain_two, shift_two)
     second_bf = normed_two.astype(jnp.bfloat16)
@@ -172,36 +179,25 @@
     )
     activ, slope = gelu_pair(pre_act)
     hidden = activ.astype(jnp.bfloat16)
-    mlp_sum = lax.psum(contract_last(hidden, down_full), "tp")
+    mlp_sum = sum_tp(contract_last(hidden, down_full))
     result = jnp.where(live_rows, resid + mlp_sum + bias_down, 0.0)
-    again = (
-        lax.all_gather(w_qkv, ("shard", "ctx"), axis=1, tiled=True),
-        lax.all_gather(w_out, ("shard", "ctx"), axis=0, tiled=True),
-        lax.all_gather(w_up, ("shard", "ctx"), axis=0, tiled=True),
-        lax.all_gather(w_down, ("shard", "ctx"), axis=0, tiled=True),
-    )
-    qkv_back, out_back, up_back, down_back = again
     grad_rows = jnp.where(live_rows, cotangent.reshape(row_count, width).astype(jnp.float32), 0.0)
     grad_bf = grad_rows.astype(jnp.bfloat16)
     grad_bias_down = jnp.sum(grad_rows, axis=0)
     grad_down = contract_first(grad_bf, hidden)
-    d_pre = jnp.dot(grad_bf, down_back, preferred_element_type=jnp.float32) * slope
+    d_pre = jnp.dot(grad_bf, down_full, preferred_element_type=jnp.float32) * slope
     d_pre_bf = d_pre.astype(jnp.bfloat16)
     grad_bias_up = jnp.sum(d_pre, axis=0)
     grad_up = contract_first(second_bf, d_pre_bf)
-    back_two = lax.psum(contract_last(d_pre_bf, up_back), "tp")
+    back_two = sum_tp(contract_last(d_pre_bf, up_full))
     grad_gain_two = jnp.sum(back_two * unit_two, axis=0)
     grad_shift_two = jnp.sum(back_two, axis=0)
     d_resid = grad_rows + normalize_back(back_two, unit_two, inv_two, gain_two)
     d_resid_bf = d_resid.astype(jnp.bfloat16)
     grad_bias_out = jnp.sum(d_resid, axis=0)
     grad_out = contract_first(d_resid_bf, attended)
-    d_attended = jnp.dot(d_resid_bf, out_back, preferred_element_type=jnp.float32).astype(
+    d_attended = jnp.dot(d_resid_bf, out_full, preferred_element_type=jnp.float32).astype(
         jnp.bfloat16
-    )
-    keys_whole, values_whole = (
-        lax.all_gather(keys_here, "ctx", axis=1, tiled=True),
-        lax.all_gather(values_here, "ctx", axis=1, tiled=True),
     )
     seq_len = keys_whole.shape[1]
     key_heads = keys_whole.reshape(groups, seq_len, heads_here, HD)
@@ -233,28 +229,27 @@
     value_terms = jnp.einsum(
         "shqk,sqhd->skhd", probs_bf, d_att_heads, preferred_element_type=jnp.float32
     )
-    d_keys, d_values = (
-        lax.psum_scatter(
-            key_terms.reshape(groups, seq_len, head_width), "ctx", scatter_dimension=1, tiled=True
-        ),
-        lax.psum_scatter(
-            value_terms.reshape(groups, seq_len, head_width), "ctx", scatter_dimension=1, tiled=True
-        ),
-    )
+    kv_terms = jnp.concatenate(
+        [
+            key_terms.reshape(groups, seq_len, head_width).astype(jnp.bfloat16),
+            value_terms.reshape(groups, seq_len, head_width).astype(jnp.bfloat16),
+        ],
+        -1,
+    )
+    kv_sum = lax.psum_scatter(kv_terms, "ctx", scatter_dimension=1, tiled=True).astype(jnp.float32)
+    d_keys, d_values = kv_sum[..., :head_width], kv_sum[..., head_width:]
     d_query_rows = d_query.reshape(row_count, head_width)
     d_value_rows = d_values.reshape(row_count, head_width)
     grad_bias_qv = jnp.stack([jnp.sum(d_query_rows, axis=0), jnp.sum(d_value_rows, axis=0)], 0)
-    stacked = jnp.stack(
-        [d_query_rows, d_keys.reshape(row_count, head_width), d_value_rows], 0
+    stacked = jnp.concatenate(
+        [d_query_rows, d_keys.reshape(row_count, head_width), d_value_rows], 1
     ).astype(jnp.bfloat16)
-    grad_qkv = jnp.einsum("rd,jre->jde", normed_bf, stacked, preferred_element_type=jnp.float32)
-    back_one = lax.psum(
-        jnp.einsum("jre,jde->rd", stacked, qkv_back, preferred_element_type=jnp.float32), "tp"
-    )
+    grad_qkv = contract_first(normed_bf, stacked)
+    back_one = sum_tp(contract_last(stacked, qkv_full))
     grad_gain_one = jnp.sum(back_one * unit_one, axis=0)
     grad_shift_one = jnp.sum(back_one, axis=0)
     d_inputs = d_resid + normalize_back(back_one, unit_one, inv_one, gain_one)
-    vec_grads = jnp.stack(
+    vec_grads = jnp.concatenate(
         [
             grad_gain_one,
             grad_shift_one,
@@ -262,18 +257,28 @@
             grad_gain_two,
             grad_shift_two,
             grad_bias_down,
-        ],
-        0,
-    )
-    summed = (
-        lax.psum_scatter(grad_qkv, ("shard", "ctx"), scatter_dimension=1, tiled=True),
-        lax.psum_scatter(grad_out, ("shard", "ctx"), scatter_dimension=0, tiled=True),
-        lax.psum_scatter(grad_up, ("shard", "ctx"), scatter_dimension=0, tiled=True),
-        lax.psum_scatter(grad_down, ("shard", "ctx"), scatter_dimension=0, tiled=True),
-        lax.psum_scatter(vec_grads, ("shard", "ctx"), scatter_dimension=1, tiled=True),
-    )
-    sum_qkv, sum_out, sum_up, sum_down, sum_vec = summed
-    bias_qv_sum, bias_up_sum = lax.psum((grad_bias_qv, grad_bias_up), ("shard", "ctx"))
+            grad_bias_qv.reshape(-1),
+            grad_bias_up,
+        ]
+    )
+    back_pair = jnp.concatenate([grad_qkv, grad_out], 1).astype(jnp.bfloat16)
+    ffn_pair = jnp.concatenate([grad_up, grad_down], 1).astype(jnp.bfloat16)
+    sum_ffn = lax.psum_scatter(
+        ffn_pair, ("shard", "ctx"), scatter_dimension=0, tiled=True
+    ).astype(jnp.float32)
+    sum_back = lax.psum_scatter(
+        back_pair, ("shard", "ctx"), scatter_dimension=0, tiled=True
+    ).astype(jnp.float32)
+    sum_qkv = jnp.stack(
+        [sum_back[:, j * head_width : (j + 1) * head_width] for j in range(3)], 0
+    )
+    sum_out = sum_back[:, qkv_width:]
+    sum_up, sum_down = sum_ffn[:, : w_up.shape[1]], sum_ffn[:, w_up.shape[1] :]
+    all_vec = lax.psum(vec_grads, ("shard", "ctx"))
+    own = lax.axis_index(("shard", "ctx")) * rows_own
+    sum_vec = lax.dynamic_slice(all_vec[: 6 * width].reshape(6, width), (0, own), (6, rows_own))
+    bias_qv_sum = all_vec[6 * width : 6 * width + 2 * head_width].reshape(2, head_width)
+    bias_up_sum = all_vec[6 * width + 2 * head_width :]
     return (
         result.reshape(groups, block_len, width),
         d_inputs.reshape(groups, block_len, width),

time: 819 us -> 514 us (0.63)
  waiting for transfers between devices: 639 us -> 331 us
  local copies, waits for them, and re-layouts: 26.2 us -> 49.4 us
  matrix products: 69.5 us -> 49.9 us
  blocking collectives: 35.5 us -> 24.1 us
    reduce_scatter x7 -> x1, waiting for transfers between devices: 233 us -> 10.2 us  [on_device(): lax.psum_scatter(kv_terms, 'ctx', scatter_dimension=1, tiled=True)]
    psum x3, waiting for transfers between devices: 324 us -> 184 us  [sum_tp(): return lax.psum(part.astype(jnp.bfloat16), 'tp').astype(jnp.float32)]
    unnamed x15 -> x11, waiting for transfers between devices: 1.93 us -> 50.1 us
    unnamed x68 -> x101, local copies, waits for them, and re-layouts: 5.09 us -> 26.6 us
    all_gather x2 -> x0, blocking collectives: 21.1 us -> none  [the longest x1 10.8 us: on_device(): lax.all_gather(w_out, ('shard', 'ctx'), axis=0, tiled=True)]
    dot_general x5 -> x3, matrix products: 17.1 us -> 5.52 us  [the longest x1 2.34 us: on_device(): jnp.dot(grad_bf, down_full, preferred_element_type=jnp.float32) * slope]
    psum x1, blocking collectives: 14.4 us -> 24.1 us  [on_device(): all_vec = lax.psum(vec_grads, ('shard', 'ctx'))]
    concatenate x0 -> x5, other arithmetic: none -> 9.6 us  [the longest x1 3.01 us: on_device(): jnp.concatenate([key_terms.reshape(groups, seq_len, head_width).astype(jn...]
  transfers between devices with their start and end apart: 15 -> 9, of which waited for: 14 -> 9; matrix products, arithmetic and copies ran while one was open for 9% -> 12% of each run, Pallas kernels for 0% -> 0%
where the time goes in v1:
time: 514 us; the launch traced here: 505 us
  waiting for transfers between devices  331 us (64%)
  matrix products  49.9 us (10%)
  local copies, waits for them, and re-layouts  49.4 us (10%)
  other arithmetic  34.7 us (7%)
  blocking collectives  24.1 us (5%)
  between operations  15.1 us (3%)
    psum x3, waiting for transfers between devices, sum_tp(): return lax.psum(part.astype(jnp.bfloat16), 'tp').astype(jnp.float32)  184 us
    unnamed x11, waiting for transfers between devices  50.1 us
    all_gather x1, waiting for transfers between devices, on_device(): whole_two = lax.all_gather(packed_two, ('shard', 'ctx'), axis=0, tiled=True)  34.7 us
    all_gather x1, waiting for transfers between devices, on_device(): whole_one = lax.all_gather(packed_one, ('shard', 'ctx'), axis=0, tiled=True)  29.9 us
    unnamed x101, local copies, waits for them, and re-layouts  26.6 us
    psum x1, blocking collectives, on_device(): all_vec = lax.psum(vec_grads, ('shard', 'ctx'))  24.1 us
    all_gather x1, waiting for transfers between devices, on_device(): lax.all_gather(jnp.concatenate([keys_here, values_here], -1), 'ctx', axis...  21.6 us
    dot_general x4, matrix products, contract_last(): lax.dot_general(left, right, (((1,), (1,)), ((), ())), preferred_element_...  13.3 us
  transfers between devices with their start and end apart: 9, of which 9 were waited for; matrix products, arithmetic and copies ran while one was open for 12% of the time, Pallas kernels for 0%

profile of v1, /device:TPU:0, one launch (start us, length us, event | category | flops | bytes accessed | tf_op | source)
XLA Modules:
  0.0 505.2 jit_solution(11412760195755958644)
XLA Ops:
  12.4 1.4 convert_reduce_fusion.2
  14.3 29.9 %all-gather.4.cloned.1.call-done = bf16[1024,1152]{1,0:T(8,128)(2,1)} async-done(((bf16[128,1152]{1,0:T(8,128)(2,1)}), bf16[1024,1152]{1,0:T(8,128)(2,1)}) %all-gather.4.cloned.1.call-update) | async-done | bytes 2359312 | tf_op jit(solution)/shard_map/all_gather | solution.py:86
  44.2 1.0 convert_bitcast_fusion
  45.2 1.6 slice_reduce_fusion
  47.3 1.0 fusion.56
  50.5 21.6 %all-gather.6.cloned.1.call-done = bf16[2,1024,512]{2,1,0:T(8,128)(2,1)} async-done(((bf16[2,256,512]{2,1,0:T(8,128)(2,1)}), bf16[2,1024,512]{2,1,0:T(8,128)(2,1)}) %all-gather.6.cloned.1.call-update) | async-done | bytes 2097168 | tf_op jit(solution)/shard_map/all_gather | solution.py:124
  72.1 3.0 fusion.82
  75.1 1.5 copy.61
  76.5 2.3 copy.59
  78.8 1.7 fusion
  80.6 3.0 select_reduce_fusion
  83.8 2.6 fusion.62
  87.1 2.6 convolution_convert_fusion.4
  89.7 1.9 pad_maximum_fusion.5
  91.9 1.3 fusion.37
  93.2 48.4 %all-reduce.6.cloned.1.call-done = bf16[512,1024]{1,0:T(8,128)(2,1)} async-done(((bf16[512,1024]{1,0:T(8,128)(2,1)}), bf16[512,1024]{1,0:T(8,128)(2,1)}) %all-reduce.6.cloned.1.call-update) | async-done | bytes 1048592 | tf_op jit(solution)/shard_map/psum | solution.py:55
  141.6 1.7 fusion.63
  144.0 1.6 add_convert_fusion
  145.5 34.7 %all-gather.8.cloned.1.call-done = bf16[1024,2048]{1,0:T(8,128)(2,1)} async-done(((bf16[128,2048]{1,0:T(8,128)(2,1)}), bf16[1024,2048]{1,0:T(8,128)(2,1)}) %all-gather.8.cloned.1.call-update) | async-done | bytes 4194320 | tf_op jit(solution)/shard_map/all_gather | solution.py:87
  180.3 3.3 fusion.44
  183.7 2.3 fusion.86
  186.1 1.0 copy-done.37
  187.1 2.3 fusion.46
  189.6 51.7 %all-reduce.8.cloned.1.call-done = bf16[512,1024]{1,0:T(8,128)(2,1)} async-done(((bf16[512,1024]{1,0:T(8,128)(2,1)}), bf16[512,1024]{1,0:T(8,128)(2,1)}) %all-reduce.8.cloned.1.call-update) | async-done | bytes 1048592 | tf_op jit(solution)/shard_map/psum | solution.py:55
  241.3 2.6 fusion.27
  243.9 1.4 fusion.80
  245.3 1.3 copy-done.3
  246.6 2.2 convolution_convert_fusion.6
  248.8 2.0 reshape.270
  250.8 2.0 copy.65
  252.8 1.1 multiply_reduce_fusion.1
  253.9 6.5 %fusion.52 = bf16[2,4,64,1024]{3,2,1,0:T(8,128)(2,1)} fusion(bf16[2,256,4,64]{1,3,2,0:T(8,128)(2,1)} %copy.65, f32[2,4,256,1024]{3,2,1,0:T(8,128)} %copy-done.2, f32[2,4,256]{2,1,0:T(4,128)S(1)} %log_add_fusion, pred[2,256,1024]{2,1,0:T(8,128)(4,1)} %copy-done.9), kind=kOutput, calls=%fused_computation.80 | convolution fusion | flops 277348352 | bytes 10231808 | tf_op jit(solution)/shard_map/shqk,sqhd->skhd/dot_general | solution.py:229
  260.5 5.5 %multiply_convert_fusion = bf16[2,4,256,1024]{3,2,1,0:T(8,128)(2,1)S(1)} fusion(f32[2,4,256,1024]{3,2,1,0:T(8,128)} %copy-done.2, f32[2,4,256]{2,1,0:T(4,128)S(1)} %bitcast.162, f32[2,4,256]{2,1,0:T(4,128)S(1)} %log_add_fusion, pred[2,256,1024]{2,1,0:T(8,128)(4,1)S(1)} %copy-done.10, bf16[2,256,4,64]{1,3,2,0:T(8,128)(2,1)S(1)} %copy-done.17, ...), kind=kOutput, calls=%fused_computation | convolution fusion | flops 281018368 | bytes 14434304 | tf_op jit(solution)/shard_map/sqhd,skhd->shqk/dot_general | solution.py:216
  266.0 2.3 multiply_convert_fusion.1
  268.3 2.3 copy.70
  270.6 2.3 copy.71
  272.9 3.0 pad_maximum_fusion.1
  276.0 3.0 convolution_convert_fusion.1
  279.0 1.6 convolution_convert_fusion
  280.6 2.4 pad_maximum_fusion
  283.0 6.6 %copy.80 = bf16[1024,2048]{1,0:T(8,128)(2,1)} copy(bf16[1024,2048]{0,1:T(8,128)(2,1)} %pad_maximum_fusion) | data formatting | bytes 8388608
  289.9 4.9 fusion.49
  294.8 1.5 fusion.84
  296.6 10.2 %reduce-scatter.8.cloned.1.call-done = bf16[2,256,512]{2,1,0:T(8,128)(2,1)} async-done(((bf16[2,1024,512]{2,1,0:T(8,128)(2,1)}), bf16[2,256,512]{2,1,0:T(8,128)(2,1)}) %reduce-scatter.8.cloned.1.call-update) | async-done | bytes 524304 | tf_op jit(solution)/shard_map/reduce_scatter | solution.py:239
  306.9 1.1 fusion.85
  308.2 3.5 convolution_convert_fusion.3
  311.9 2.1 convolution_convert_fusion.5
  314.1 1.0 convolution_convert_fusion.2
  315.1 1.5 pad_maximum_fusion.2
  316.6 4.0 copy.78
  320.7 1.3 copy-done.8
  322.4 1.1 convert_reduce_fusion.3
  323.5 38.5 %reduce-scatter.12.cloned.1.call-done = bf16[128,2048]{1,0:T(8,128)(2,1)} async-done(((bf16[1024,2048]{1,0:T(8,128)(2,1)}), bf16[128,2048]{1,0:T(8,128)(2,1)}) %reduce-scatter.12.cloned.1.call-update) | async-done | bytes 524304
  362.0 1.3 copy.81
  363.3 0.9 fusion.83
  364.2 2.0 copy.77
  366.2 1.0 copy.76
  367.2 84.3 %all-reduce.10.cloned.1.call-done = (bf16[512,1024]{1,0:T(8,128)(2,1)}, bf16[512,1024]{1,0:T(8,128)(2,1)}) async-done(((bf16[512,1024]{1,0:T(8,128)(2,1)}, bf16[512,1024]{1,0:T(8,128)(2,1)}), (bf16[512,1024]{1,0:T(8,128)(2,1)}, bf16[512,1024]{1,0:T(8,128)(2,1)})) %all-reduce.10.cloned.1.call-update) | async-done | bytes 2097168 | tf_op jit(solution)/shard_map/psum | solution.py:55
  451.5 2.3 fusion.28
  453.9 24.1 %psum.39 = f32[7680]{0:T(1024)S(1)} all-reduce(f32[7680]{0:T(1024)S(1)} %constant_dynamic-update-slice_fusion.3), channel_id=1, replica_groups=mesh['shard'=2,'ctx'=4,'tp'=4] {'shard','ctx'}, use_global_device_ids=true, to_apply=%region_25.26 | all-reduce | flops 7680 | bytes 61440 | tf_op jit(solution)/shard_map/psum | solution.py:277
  479.8 4.1 fusion.15
  483.8 11.5 %reduce-scatter.10.cloned.1.call-done = bf16[128,1024]{1,0:T(8,128)(2,1)} async-done(((bf16[1024,1024]{1,0:T(8,128)(2,1)}), bf16[128,1024]{1,0:T(8,128)(2,1)}) %reduce-scatter.10.cloned.1.call-update) | async-done | bytes 262160
  495.3 1.1 copy.79
  497.3 0.9 copy.74
  (155 shorter events, 14.6 us)
Async XLA Ops:
  7.2 6.7 %copy-start = (bf16[2,256,1024]{2,1,0:T(8,128)(2,1)S(1)}, bf16[2,256,1024]{2,1,0:T(8,128)(2,1)}, u32[]{:S(2)}) copy-start(bf16[2,256,1024]{2,1,0:T(8,128)(2,1)} %param.15) | copy-start | bytes 3145732
  7.2 7.1 %copy-start.31 = (bf16[2,256]{1,0:T(2,128)(2,1)S(1)}, bf16[2,256]{1,0:T(2,128)(2,1)}, u32[]{:S(2)}) copy-start(bf16[2,256]{1,0:T(2,128)(2,1)} %param.21) | copy-start | bytes 3076
  7.2 37.0 %all-gather.4.cloned.1.call-start = ((), (), s32[]{:S(2)}) async-start(), calls=%async_computation.3 | async-start | bytes 2654208 | tf_op jit(solution)/shard_map/all_gather | solution.py:86
  11.6 0.7 copy-start.24
  12.4 59.7 %all-gather.6.cloned.1.call-start = ((), (), s32[]{:S(2)}) async-start(), calls=%async_computation.4 | async-start | bytes 2621440 | tf_op jit(solution)/shard_map/all_gather | solution.py:124
  45.2 2.0 copy-start.23
  47.3 1.0 copy-start.18
  48.3 1.1 copy-start.33
  49.3 92.3 %all-reduce.6.cloned.1.call-start = ((), (), s32[]{:S(2)}) async-start(), calls=%async_computation.5 | async-start | bytes 2097152 | tf_op jit(solution)/shard_map/psum | solution.py:55
  49.9 33.6 %copy-start.9 = (pred[2,256,1024]{2,1,0:T(8,128)(4,1)}, pred[2,256,1024]{2,1,0:T(8,128)(4,1)S(1)}, u32[]{:S(2)}) copy-start(pred[2,256,1024]{2,1,0:T(8,128)(4,1)S(1)} %broadcast_and_fusion) | copy-start | bytes 1572868
  50.5 28.4 %copy-start.13 = (bf16[2,256,4,64]{1,3,2,0:T(8,128)(2,1)}, bf16[2,256,4,64]{1,3,2,0:T(8,128)(2,1)S(1)}, u32[]{:S(2)}) copy-start(bf16[2,256,4,64]{1,3,2,0:T(8,128)(2,1)S(1)} %copy.62) | copy-start | bytes 786436
  80.5 3.2 copy-start.2
  80.6 3.2 copy-start.20
  86.4 0.7 copy-start.22
  87.1 4.9 copy-start.32
  87.1 4.9 copy-start.6
  89.7 90.6 %all-gather.8.cloned.1.call-start = ((), (), s32[]{:S(2)}) async-start(), calls=%async_computation.6 | async-start | bytes 4718592 | tf_op jit(solution)/shard_map/all_gather | solution.py:87
  91.6 149.7 %all-reduce.8.cloned.1.call-start = ((), (), s32[]{:S(2)}) async-start(), calls=%async_computation.7 | async-start | bytes 2097152 | tf_op jit(solution)/shard_map/psum | solution.py:55
  141.6 1.7 copy-start.1
  180.3 3.3 copy-start.15
  180.3 3.5 copy-start.34
  183.7 2.4 copy-start.35
  186.1 1.0 copy-start.37
  189.3 117.5 %reduce-scatter.8.cloned.1.call-start = ((), (), s32[]{:S(2)}) async-start(), calls=%async_computation.8 | async-start | bytes 2621440 | tf_op jit(solution)/shard_map/reduce_scatter | solution.py:239
  241.3 2.6 copy-start.7
  241.3 2.6 copy-start.12
  245.3 1.3 copy-start.3
  253.9 6.6 %copy-start.10 = (pred[2,256,1024]{2,1,0:T(8,128)(4,1)S(1)}, pred[2,256,1024]{2,1,0:T(8,128)(4,1)}, u32[]{:S(2)}) copy-start(pred[2,256,1024]{2,1,0:T(8,128)(4,1)} %copy-done.9) | copy-start | bytes 1572868
  253.9 6.6 %copy-start.17 = (bf16[2,256,4,64]{1,3,2,0:T(8,128)(2,1)S(1)}, bf16[2,256,4,64]{1,3,2,0:T(8,128)(2,1)}, u32[]{:S(2)}) copy-start(bf16[2,256,4,64]{1,3,2,0:T(8,128)(2,1)} %copy.65) | copy-start | bytes 786436
  253.9 6.6 %copy-start.21 = (bf16[2,1024,256]{1,2,0:T(8,128)(2,1)S(1)}, bf16[2,1024,256]{1,2,0:T(8,128)(2,1)}, u32[]{:S(2)}) copy-start(bf16[2,1024,256]{1,2,0:T(8,128)(2,1)} %copy.59) | copy-start | bytes 3145732
  260.5 5.5 %copy-start.14 = (bf16[2,256,4,64]{1,3,2,0:T(8,128)(2,1)S(1)}, bf16[2,256,4,64]{1,3,2,0:T(8,128)(2,1)}, u32[]{:S(2)}) copy-start(bf16[2,256,4,64]{1,3,2,0:T(8,128)(2,1)} %copy-done.13) | copy-start | bytes 786436
  266.0 2.3 copy-start.4
  275.9 86.1 %reduce-scatter.12.cloned.1.call-start = ((), (), s32[]{:S(2)}) async-start(), calls=%async_computation.10 | async-start | bytes 4718592
  276.0 3.0 copy-start.16
  276.0 3.0 copy-start.36
  289.6 161.9 %all-reduce.10.cloned.1.call-start = ((), (), s32[]{:S(2)}) async-start(), calls=%async_computation.11 | async-start | bytes 4194304 | tf_op jit(solution)/shard_map/psum | solution.py:55
  289.9 4.9 copy-start.5
  296.6 15.1 %copy-start.25 = (bf16[32,8,2,256]{3,1,2,0:T(8,128)(2,1)}, bf16[32,8,2,256]{3,1,2,0:T(8,128)(2,1)S(1)}, u32[]{:S(2)}) copy-start(bf16[32,8,2,256]{3,1,2,0:T(8,128)(2,1)S(1)} %copy.90) | copy-start | bytes 786436
  308.1 3.7 copy-start.27
  308.2 3.5 copy-start.29
  311.8 2.3 copy-start.19
  311.8 183.5 %reduce-scatter.10.cloned.1.call-start = ((), (), s32[]{:S(2)}) async-start(), calls=%async_computation.9 | async-start | bytes 2359296
  311.9 2.2 copy-start.26
  311.9 2.2 copy-start.28
  311.9 2.2 copy-start.30
  320.6 1.3 copy-start.8
  451.5 28.3 %copy-start.11 = (bf16[512,1024]{1,0:T(8,128)(2,1)S(1)}, bf16[512,1024]{1,0:T(8,128)(2,1)}, u32[]{:S(2)}) copy-start(bf16[512,1024]{1,0:T(8,128)(2,1)} %get-tuple-element.71) | copy-start | bytes 3145732
Sparse Core Ops, SparseCore 0:
  12.5 31.7 all-gather.3
  49.4 22.5 all-gather.5
  89.8 51.8 all-reduce.5
  144.1 36.0 all-gather.7
  189.5 51.7 all-reduce.7
  276.0 30.7 reduce-scatter.7
  310.6 51.3 reduce-scatter.11
  364.4 87.0 all-reduce.9
  455.1 40.1 reduce-scatter.9

commit v2 on v1

--- a/solution.py
+++ b/solution.py
@@ -1,8 +1,11 @@
+import functools
 import math
 
 import jax
 import jax.numpy as jnp
 from jax import lax
+from jax.experimental import pallas as pl
+from jax.experimental.pallas import tpu as pltpu
 from jax.sharding import PartitionSpec as P
 
 HD = 64
@@ -51,11 +54,247 @@
     )
 
 
-def sum_tp(part):
-    return lax.psum(part.astype(jnp.bfloat16), "tp").astype(jnp.float32)
+MESH = pl.DeviceIdType.MESH
+VMEM_SPEC = pl.BlockSpec(memory_space=pltpu.VMEM)
+
+
+def remote(src, dst, send_sem, recv_sem, device):
+    return pltpu.make_async_remote_copy(
+        src_ref=src,
+        dst_ref=dst,
+        send_sem=send_sem,
+        recv_sem=recv_sem,
+        device_id=device,
+        device_id_type=MESH,
+    )
+
+
+def greet(devices):
+    barrier = pltpu.get_barrier_semaphore()
+    for device in devices:
+        pl.semaphore_signal(barrier, inc=1, device_id=device, device_id_type=MESH)
+    pl.semaphore_wait(barrier, len(devices))
+
+
+def params(collective_id):
+    return pltpu.CompilerParams(
+        collective_id=collective_id, has_side_effects=True, vmem_limit_bytes=48 * 2**20
+    )
+
+
+def dma_sems(*counts):
+    return [pltpu.SemaphoreType.DMA((count,)) for count in counts]
+
+
+def tp_kernel(n, x_ref, out_ref, recv, send_one, recv_one, send_two, recv_two):
+    me = lax.axis_index("tp")
+    rows = x_ref.shape[0] // n
+    peers = [lax.rem(me + k, n) for k in range(1, n)]
+
+    def share(index):
+        return pl.ds(pl.multiple_of(index * rows, rows), rows)
+
+    greet([{"tp": peer} for peer in peers])
+    first = [
+        remote(x_ref.at[share(peer)], recv.at[k], send_one.at[k], recv_one.at[k], {"tp": peer})
+        for k, peer in enumerate(peers)
+    ]
+    for copy in first:
+        copy.start()
+    total = x_ref[share(me), :].astype(jnp.float32)
+    for k, copy in enumerate(first):
+        copy.wait_recv()
+        total = total + recv[k].astype(jnp.float32)
+    out_ref[share(me), :] = total.astype(out_ref.dtype)
+    second = [
+        remote(
+            out_ref.at[share(me)], out_ref.at[share(me)], send_two.at[k], recv_two.at[k], {"tp": peer}
+        )
+        for k, peer in enumerate(peers)
+    ]
+    for copy in second:
+        copy.start()
+    for copy in first:
+        copy.wait_send()
+    for copy in second:
+        copy.wait()
+
+
+def sum_tp(part, n):
+    part = part.astype(jnp.bfloat16)
+    rows, width = part.shape
+    total = pl.pallas_call(
+        functools.partial(tp_kernel, n),
+        out_shape=jax.ShapeDtypeStruct(part.shape, part.dtype),
+        in_specs=[VMEM_SPEC],
+        out_specs=VMEM_SPEC,
+        scratch_shapes=[pltpu.VMEM((n - 1, rows // n, width), part.dtype)]
+        + dma_sems(n - 1, n - 1, n - 1, n - 1),
+        compiler_params=params(1),
+        cost_estimate=pl.CostEstimate(flops=0, bytes_accessed=120_000_000, transcendentals=0),
+        name="sum_tp",
+    )(part)
+    return total.astype(jnp.float32)
+
+
+def group(shards, ctx):
+    chips_y = ctx // 2
+    place = lax.axis_index("ctx")
+    core = lax.rem(place, 2)
+    chip = place // 2
+    if shards > 1:
+        chip = chip + lax.axis_index("shard") * chips_y
+
+    def device(index):
+        where = {"ctx": lax.rem(index, chips_y) * 2 + core}
+        if shards > 1:
+            where["shard"] = index // chips_y
+        return where
+
+    return chip, core, device, {"ctx": place + 1 - 2 * core}
+
+
+def gather_kernel(shards, ctx, x_ref, out_ref, own_sem, send_sem, recv_sem):
+    chips = shards * ctx // 2
+    chip, core, device, sibling = group(shards, ctx)
+    other = 1 - core
+    targets = [device(lax.rem(chip + k, chips)) for k in range(1, chips)]
+    greet(targets + [sibling])
+    mine = chip * 2 + core
+    keep = pltpu.make_async_copy(x_ref, out_ref.at[mine], own_sem.at[0])
+    keep.start()
+    away = [
+        remote(x_ref, out_ref.at[mine], send_sem.at[k], recv_sem.at[k], target)
+        for k, target in enumerate(targets + [sibling])
+    ]
+    for copy in away:
+        copy.start()
+    onward = []
+    for k in range(1, chips):
+        away[k - 1].wait_recv()
+        source = lax.rem(chip - k + chips, chips) * 2 + core
+        copy = remote(
+            out_ref.at[source],
+            out_ref.at[source],
+            send_sem.at[chips + k - 1],
+            recv_sem.at[chips + k - 1],
+            sibling,
+        )
+        copy.start()
+        onward.append(copy)
+    away[-1].wait_recv()
+    for copy in onward:
+        copy.wait()
+    for copy in away:
+        copy.wait_send()
+    keep.wait()
+
+
+def gather(block, shards, ctx, collective_id):
+    count = shards * ctx
+    return pl.pallas_call(
+        functools.partial(gather_kernel, shards, ctx),
+        out_shape=jax.ShapeDtypeStruct((count,) + block.shape, block.dtype),
+        in_specs=[VMEM_SPEC],
+        out_specs=VMEM_SPEC,
+        scratch_shapes=dma_sems(1, count - 1, count - 1),
+        compiler_params=params(collective_id),
+        cost_estimate=pl.CostEstimate(flops=0, bytes_accessed=40_000_000, transcendentals=0),
+        name="gather_blocks",
+    )(block)
+
+
+def scatter_kernel(shards, ctx, x_ref, out_ref, pair, held, send_sem, recv_sem, pair_send, pair_recv):
+    chips = shards * ctx // 2
+    chip, core, device, sibling = group(shards, ctx)
+    other = 1 - core
+    targets = [device(lax.rem(chip + k, chips)) for k in range(1, chips)]
+    greet(targets + [sibling])
+    order = [lax.rem(chip + k, chips) for k in range(1, chips)] + [chip]
+    swaps = [
+        remote(
+            x_ref.at[owner * 2 + other], pair.at[k], pair_send.at[k], pair_recv.at[k], sibling
+        )
+        for k, owner in enumerate(order)
+    ]
+    for copy in swaps:
+        copy.start()
+    away = []
+    for k, owner in enumerate(order):
+        swaps[k].wait_recv()
+        both = x_ref[owner * 2 + core].astype(jnp.float32) + pair[k].astype(jnp.float32)
+        if k < chips - 1:
+            pair[k] = both.astype(pair.dtype)
+            copy = remote(pair.at[k], held.at[k], send_sem.at[k], recv_sem.at[k], targets[k])
+            copy.start()
+            away.append(copy)
+        else:
+            out_ref[...] = both
+    for k, copy in enumerate(away):
+        copy.wait_recv()
+        out_ref[...] += held[k].astype(jnp.float32)
+    for copy in away + swaps:
+        copy.wait_send()
+
+
+def scatter(blocks, shards, ctx, collective_id):
+    count = shards * ctx
+    chips = count // 2
+    shape = blocks.shape[1:]
+    return pl.pallas_call(
+        functools.partial(scatter_kernel, shards, ctx),
+        out_shape=jax.ShapeDtypeStruct(shape, jnp.float32),
+        in_specs=[VMEM_SPEC],
+        out_specs=VMEM_SPEC,
+        scratch_shapes=[
+            pltpu.VMEM((chips,) + shape, blocks.dtype),
+            pltpu.VMEM((chips - 1,) + shape, blocks.dtype),
+        ]
+        + dma_sems(chips - 1, chips - 1, chips, chips),
+        compiler_params=params(collective_id),
+        cost_estimate=pl.CostEstimate(flops=0, bytes_accessed=40_000_000, transcendentals=0),
+        name="scatter_blocks",
+    )(blocks)
+
+
+def small_kernel(shards, ctx, x_ref, out_ref, held, send_sem, recv_sem):
+    count = shards * ctx
+    me = lax.axis_index("shard") * ctx + lax.axis_index("ctx")
+    peers = [lax.rem(me + k, count) for k in range(1, count)]
+    targets = [{"shard": peer // ctx, "ctx": lax.rem(peer, ctx)} for peer in peers]
+    greet(targets)
+    copies = [
+        remote(x_ref, held.at[k], send_sem.at[k], recv_sem.at[k], target)
+        for k, target in enumerate(targets)
+    ]
+    for copy in copies:
+        copy.start()
+    out_ref[...] = x_ref[...]
+    for k, copy in enumerate(copies):
+        copy.wait_recv()
+        out_ref[...] += held[k]
+    for copy in copies:
+        copy.wait_send()
+
+
+def small_sum(part, shards, ctx, collective_id):
+    count = shards * ctx
+    return pl.pallas_call(
+        functools.partial(small_kernel, shards, ctx),
+        out_shape=jax.ShapeDtypeStruct(part.shape, part.dtype),
+        in_specs=[VMEM_SPEC],
+        out_specs=VMEM_SPEC,
+        scratch_shapes=[pltpu.VMEM((count - 1,) + part.shape, part.dtype)]
+        + dma_sems(count - 1, count - 1),
+        compiler_params=params(collective_id),
+        name="small_sum",
+    )(part)
 
 
 def on_device(
+    shards,
+    ctx,
+    tp,
     hidden_in,
     lengths,
     cotangent,
@@ -83,7 +322,7 @@
         [w_qkv[0], w_qkv[1], w_qkv[2], w_out, jnp.pad(vectors, ((0, 0), (0, 122)))], 1
     )
     packed_two = jnp.concatenate([w_up, w_down], 1)
-    whole_one = lax.all_gather(packed_one, ("shard", "ctx"), axis=0, tiled=True)
+    whole_one = gather(packed_one, shards, ctx, 2).reshape(-1, packed_one.shape[1])
     whole_two = lax.all_gather(packed_two, ("shard", "ctx"), axis=0, tiled=True)
     qkv_width = 3 * head_width
     qkv_full = whole_one[:, :qkv_width]
@@ -121,8 +360,13 @@
     )
     query_heads = query.reshape(groups, block_len, heads_here, HD)
 
-    kv_whole = lax.all_gather(
-        jnp.concatenate([keys_here, values_here], -1), "ctx", axis=1, tiled=True
+    kv_blocks = gather(
+        jnp.concatenate([keys_here, values_here], -1).reshape(row_count, 2 * head_width), 1, ctx, 3
+    )
+    kv_whole = (
+        kv_blocks.reshape(ctx, groups, block_len, 2 * head_width)
+        .transpose(1, 0, 2, 3)
+        .reshape(groups, ctx * block_len, 2 * head_width)
     )
     keys_whole, values_whole = kv_whole[..., :head_width], kv_whole[..., head_width:]
 
@@ -170,7 +414,7 @@
     accum = fold_keys(values_step, jnp.zeros((groups, block_len, heads_here, HD), jnp.float32))
     attended_heads = accum.astype(jnp.bfloat16)
     attended = attended_heads.reshape(row_count, head_width)
-    proj_sum = sum_tp(contract_last(attended, out_full))
+    proj_sum = sum_tp(contract_last(attended, out_full), tp)
     resid = inputs + proj_sum + bias_out
     normed_two, unit_two, inv_two = normalize(resid, gain_two, shift_two)
     second_bf = normed_two.astype(jnp.bfloat16)
@@ -179,7 +423,9 @@
     )
     activ, slope = gelu_pair(pre_act)
     hidden = activ.astype(jnp.bfloat16)
-    mlp_sum = sum_tp(contract_last(hidden, down_full))
+    mlp_sum = lax.psum(contract_last(hidden, down_full).astype(jnp.bfloat16), "tp").astype(
+        jnp.float32
+    )
     result = jnp.where(live_rows, resid + mlp_sum + bias_down, 0.0)
     grad_rows = jnp.where(live_rows, cotangent.reshape(row_count, width).astype(jnp.float32), 0.0)
     grad_bf = grad_rows.astype(jnp.bfloat16)
@@ -189,7 +435,7 @@
     d_pre_bf = d_pre.astype(jnp.bfloat16)
     grad_bias_up = jnp.sum(d_pre, axis=0)
     grad_up = contract_first(second_bf, d_pre_bf)
-    back_two = sum_tp(contract_last(d_pre_bf, up_full))
+    back_two = sum_tp(contract_last(d_pre_bf, up_full), tp)
     grad_gain_two = jnp.sum(back_two * unit_two, axis=0)
     grad_shift_two = jnp.sum(back_two, axis=0)
     d_resid = grad_rows + normalize_back(back_two, unit_two, inv_two, gain_two)
@@ -236,16 +482,21 @@
         ],
         -1,
     )
-    kv_sum = lax.psum_scatter(kv_terms, "ctx", scatter_dimension=1, tiled=True).astype(jnp.float32)
+    kv_blocks_grad = (
+        kv_terms.reshape(groups, ctx, block_len, 2 * head_width)
+        .transpose(1, 0, 2, 3)
+        .reshape(ctx, row_count, 2 * head_width)
+    )
+    kv_sum = scatter(kv_blocks_grad, 1, ctx, 4)
     d_keys, d_values = kv_sum[..., :head_width], kv_sum[..., head_width:]
     d_query_rows = d_query.reshape(row_count, head_width)
     d_value_rows = d_values.reshape(row_count, head_width)
     grad_bias_qv = jnp.stack([jnp.sum(d_query_rows, axis=0), jnp.sum(d_value_rows, axis=0)], 0)
     stacked = jnp.concatenate(
-        [d_query_rows, d_keys.reshape(row_count, head_width), d_value_rows], 1
+        [d_query_rows, d_keys, d_value_rows], 1
     ).astype(jnp.bfloat16)
     grad_qkv = contract_first(normed_bf, stacked)
-    back_one = sum_tp(contract_last(stacked, qkv_full))
+    back_one = sum_tp(contract_last(stacked, qkv_full), tp)
     grad_gain_one = jnp.sum(back_one * unit_one, axis=0)
     grad_shift_one = jnp.sum(back_one, axis=0)
     d_inputs = d_resid + normalize_back(back_one, unit_one, inv_one, gain_one)
@@ -274,7 +525,7 @@
     )
     sum_out = sum_back[:, qkv_width:]
     sum_up, sum_down = sum_ffn[:, : w_up.shape[1]], sum_ffn[:, w_up.shape[1] :]
-    all_vec = lax.psum(vec_grads, ("shard", "ctx"))
+    all_vec = small_sum(vec_grads.reshape(-1, 128), shards, ctx, 5).reshape(-1)
     own = lax.axis_index(("shard", "ctx")) * rows_own
     sum_vec = lax.dynamic_slice(all_vec[: 6 * width].reshape(6, width), (0, own), (6, rows_own))
     bias_qv_sum = all_vec[6 * width : 6 * width + 2 * head_width].reshape(2, head_width)
@@ -299,7 +550,9 @@
 
 def solution(mesh):
     return jax.shard_map(
-        on_device,
+        functools.partial(
+            on_device, mesh.shape["shard"], mesh.shape["ctx"], mesh.shape["tp"]
+        ),
         mesh=mesh,
         in_specs=(
             P("shard", "ctx", None),

time: 514 us -> 414 us (0.81)
  waiting for transfers between devices: 331 us -> 32.5 us
  Pallas kernels: 0 us -> 229 us
  blocking collectives: 24.1 us -> 0 us
    pallas_call x0 -> x7, Pallas kernels: none -> 229 us  [the longest x3 162 us: sum_tp(): pl.pallas_call(functools.partial(tp_kernel, n), out_shape=jax.ShapeDtypeS...]
    psum x3 -> x1, waiting for transfers between devices: 184 us -> 11.4 us  [on_device(): lax.psum(contract_last(hidden, down_full).astype(jnp.bfloat16), 'tp')]
    all_gather x2 -> x0, waiting for transfers between devices: 51.5 us -> none  [the longest x1 29.9 us: on_device(): whole_one = lax.all_gather(packed_one, ('shard', 'ctx'), axis=0, tiled=True)]
    all_gather x1, waiting for transfers between devices: 34.7 us -> 0.02 us  [on_device(): whole_two = lax.all_gather(packed_two, ('shard', 'ctx'), axis=0, tiled=True)]
    unnamed x11 -> x6, waiting for transfers between devices: 50.1 us -> 21 us
    psum x1 -> x0, blocking collectives: 24.1 us -> none  [on_device(): all_vec = lax.psum(vec_grads, ('shard', 'ctx'))]
    reduce_scatter x1 -> x0, waiting for transfers between devices: 10.2 us -> none  [on_device(): lax.psum_scatter(kv_terms, 'ctx', scatter_dimension=1, tiled=True)]
    dot_general x4, matrix products: 13.3 us -> 6.36 us  [contract_last(): lax.dot_general(left, right, (((1,), (1,)), ((), ())), preferred_element_...]
  transfers between devices with their start and end apart: 9 -> 4, of which waited for: 9 -> 2; matrix products, arithmetic and copies ran while one was open for 12% -> 16% of each run, Pallas kernels for 0% -> 52%
where the time goes in v2:
time: 414 us; the launch traced here: 406 us
  Pallas kernels  229 us (55%)
  local copies, waits for them, and re-layouts  50.3 us (12%)
  matrix products  47 us (11%)
  waiting for transfers between devices  32.5 us (8%)
  other arithmetic  32.3 us (8%)
  between operations  15.1 us (4%)
    pallas_call x3, Pallas kernels, sum_tp(): pl.pallas_call(functools.partial(tp_kernel, n), out_shape=jax.ShapeDtypeS...  162 us
    pallas_call x2, Pallas kernels, gather(): pl.pallas_call(functools.partial(gather_kernel, shards, ctx), out_shape=j...  43 us
    unnamed x100, local copies, waits for them, and re-layouts  23.2 us
    unnamed x6, waiting for transfers between devices  21 us
    pallas_call x1, Pallas kernels, scatter(): pl.pallas_call(functools.partial(scatter_kernel, shards, ctx), out_shape=...  16.3 us
    psum x1, waiting for transfers between devices, on_device(): lax.psum(contract_last(hidden, down_full).astype(jnp.bfloat16), 'tp')  11.4 us
    dot_general x4, matrix products, contract_first(): lax.dot_general(left, right, (((0,), (0,)), ((), ())), preferred_element_...  8.3 us
  transfers between devices with their start and end apart: 4, of which 2 were waited for; matrix products, arithmetic and copies ran while one was open for 16% of the time, Pallas kernels for 52%

profile of v2, /device:TPU:0, one launch (start us, length us, event | category | flops | bytes accessed | tf_op | source)
XLA Modules:
  0.0 406.2 jit_solution(8865236314756687385)
XLA Ops:
  7.3 1.9 pad_maximum_fusion.5
  11.1 24.3 %gather_blocks.2 = bf16[8,128,1152]{2,1,0:T(8,128)(2,1)S(1)} custom-call(bf16[128,1152]{1,0:T(8,128)(2,1)S(1)} %pad_dynamic-update-slice_fusion.x_ref), custom_call_target="tpu_custom_call" | custom-call | bytes 40000000 | tf_op jit(solution)/shard_map/gather_blocks/pallas_call | solution.py:195
  36.2 1.9 copy.101
  38.2 1.0 convert_bitcast_fusion
  39.7 1.0 fusion.56
  42.3 2.0 reshape.285
  44.3 2.0 copy.76
  46.3 1.1 pad_maximum_fusion.4.x_ref
  47.3 18.7 %gather_blocks.3 = bf16[4,512,512]{2,1,0:T(8,128)(2,1)S(1)} custom-call(bf16[512,512]{1,0:T(8,128)(2,1)S(1)} %pad_maximum_fusion.4.x_ref), custom_call_target="tpu_custom_call" | custom-call | bytes 40000000 | tf_op jit(solution)/shard_map/gather_blocks/pallas_call | solution.py:195
  66.1 1.5 fusion.86
  67.6 2.3 copy.75
  69.9 2.3 copy.73
  72.7 3.2 fusion
  76.0 3.0 select_reduce_fusion
  79.2 2.8 fusion.66
  83.1 44.4 %sum_tp.3 = bf16[512,1024]{1,0:T(8,128)(2,1)S(1)} custom-call(bf16[512,1024]{1,0:T(8,128)(2,1)S(1)} %convolution_convert_fusion.4.x_ref), custom_call_target="tpu_custom_call" | custom-call | bytes 120000000 | tf_op jit(solution)/shard_map/sum_tp/pallas_call | solution.py:126
  128.8 1.2 fusion.37
  130.7 3.2 fusion.44
  133.9 1.3 copy-done.35
  135.3 2.5 fusion.49
  137.8 5.0 %fusion.90 = (f32[1024]{0:T(1024)S(1)}, bf16[512,1024]{1,0:T(8,128)(2,1)S(1)}) fusion(f32[512,1024]{1,0:T(8,128)} %copy-done.35, f32[1024]{0:T(1024)S(1)} %convert_element_type.143, bf16[512,1024]{1,0:T(8,128)(2,1)} %fusion.37, bf16[1024,2048]{1,0:T(8,128)(2,1)} %all-gather.2.cloned.1.call-done), kind=kOutput, calls=%fused_computation.166 | convolution fusion | flops 1084750848 | bytes 6299648 | tf_op jit(solution)/shard_map/dot_general | solution.py:434
  142.8 1.0 copy-done.37
  143.8 1.3 fusion.46.x_ref
  145.1 73.1 %sum_tp.4 = bf16[512,1024]{1,0:T(8,128)(2,1)S(1)} custom-call(bf16[512,1024]{1,0:T(8,128)(2,1)S(1)} %fusion.46.x_ref), custom_call_target="tpu_custom_call" | custom-call | bytes 120000000 | tf_op jit(solution)/shard_map/sum_tp/pallas_call | solution.py:126
  218.2 1.2 fusion.27
  219.4 11.4 %all-reduce.3.cloned.1.call-done = bf16[512,1024]{1,0:T(8,128)(2,1)} async-done(((bf16[512,1024]{1,0:T(8,128)(2,1)}), bf16[512,1024]{1,0:T(8,128)(2,1)}) %all-reduce.3.cloned.1.call-update) | async-done | bytes 1048592 | tf_op jit(solution)/shard_map/psum | solution.py:426
  230.8 4.1 %fusion.84 = (f32[1024]{0:T(1024)S(1)}, f32[512,1024]{1,0:T(8,128)S(1)}, f32[512,1024]{1,0:T(8,128)}) fusion(f32[512]{0:T(512)S(1)} %get-tuple-element.99, f32[512]{0:T(512)S(1)} %broadcast_multiply_fusion.4, f32[1024]{0:T(1024)S(1)} %bitcast.174, bf16[512,1024]{1,0:T(8,128)(2,1)S(1)} %sum_tp.3, bf16[2,256,1024]{2,1,0:T(8,128)(2,1)S(1)} %copy-done.2, ...), kind=kLoop, calls=%fused_computation.161 | loop fusion | flops 10484736 | bytes 9462272 | tf_op jit(solution)/shard_map/reduce_sum | solution.py:443
  234.9 1.2 convolution_convert_fusion.5
  236.5 1.0 copy-done.1
  237.5 1.1 convolution_convert_fusion.6
  238.7 1.2 reshape.286
  239.9 1.0 copy.79
  240.9 1.1 multiply_reduce_fusion.1
  242.0 6.5 %fusion.58 = bf16[2,1024,4,64]{1,3,2,0:T(8,128)(2,1)} fusion(bf16[2,256,4,64]{1,3,2,0:T(8,128)(2,1)} %copy.79, f32[2,4,256,1024]{3,2,1,0:T(8,128)} %copy-done.4, f32[2,4,256]{2,1,0:T(4,128)S(1)} %log_add_fusion, pred[2,256,1024]{2,1,0:T(8,128)(4,1)S(1)} %copy-done.9), kind=kOutput, calls=%fused_computation.84 | convolution fusion | flops 277348352 | bytes 10231808 | tf_op jit(solution)/shard_map/shqk,sqhd->skhd/dot_general | solution.py:475
  248.5 5.5 %multiply_convert_fusion = bf16[2,4,256,1024]{3,2,1,0:T(8,128)(2,1)S(1)} fusion(f32[2,4,256,1024]{3,2,1,0:T(8,128)} %copy-done.4, f32[2,4,256]{2,1,0:T(4,128)S(1)} %bitcast.190, f32[2,4,256]{2,1,0:T(4,128)S(1)} %log_add_fusion, pred[2,256,1024]{2,1,0:T(8,128)(4,1)S(1)} %copy-done.10, bf16[2,256,4,64]{1,3,2,0:T(8,128)(2,1)S(1)} %copy-done.17, ...), kind=kOutput, calls=%fused_computation | convolution fusion | flops 281018368 | bytes 14434304 | tf_op jit(solution)/shard_map/sqhd,skhd->shqk/dot_general | solution.py:462
  254.1 2.2 fusion.88
  256.2 1.8 fusion.61
  258.1 1.9 convert_element_type.160
  259.9 1.5 copy.84
  261.4 1.9 convert_element_type.164
  263.3 1.5 copy.85
  264.7 1.7 pad_maximum_fusion.1
  266.4 16.3 %scatter_blocks.1 = f32[512,512]{1,0:T(8,128)S(1)} custom-call(bf16[4,512,512]{2,1,0:T(8,128)(2,1)S(1)} %bitcast.153), custom_call_target="tpu_custom_call" | custom-call | bytes 40000000 | tf_op jit(solution)/shard_map/scatter_blocks/pallas_call | solution.py:244
  283.6 2.0 copy.91
  285.6 2.2 reshape.280
  287.8 2.5 convolution_convert_fusion.2
  290.3 1.5 pad_maximum_fusion.2
  291.8 3.9 copy.92
  296.1 3.0 convolution_convert_fusion.1
  299.1 1.6 convolution_convert_fusion
  300.7 2.4 pad_maximum_fusion
  303.1 6.6 %copy.94 = bf16[1024,2048]{1,0:T(8,128)(2,1)} copy(bf16[1024,2048]{0,1:T(8,128)(2,1)} %pad_maximum_fusion) | data formatting | bytes 8388608
  309.7 1.5 select_reduce_fusion.1
  311.5 2.1 convolution_convert_fusion.3.x_ref
  313.6 45.0 %sum_tp.5 = bf16[512,1024]{1,0:T(8,128)(2,1)S(1)} custom-call(bf16[512,1024]{1,0:T(8,128)(2,1)S(1)} %convolution_convert_fusion.3.x_ref), custom_call_target="tpu_custom_call" | custom-call | bytes 120000000 | tf_op jit(solution)/shard_map/sum_tp/pallas_call | solution.py:126
  358.6 1.0 fusion.28
  359.7 6.8 %small_sum.1 = f32[60,128]{1,0:T(8,128)S(1)} custom-call(f32[60,128]{1,0:T(8,128)S(1)} %bitcast.159), custom_call_target="tpu_custom_call" | custom-call | tf_op jit(solution)/shard_map/small_sum/pallas_call | solution.py:282
  368.3 3.7 fusion.15
  371.9 1.1 copy.93
  373.9 0.9 copy.87
  374.8 21.0 %reduce-scatter.9.cloned.1.call-done = bf16[128,2048]{1,0:T(8,128)(2,1)} async-done(((bf16[1024,2048]{1,0:T(8,128)(2,1)}), bf16[128,2048]{1,0:T(8,128)(2,1)}) %reduce-scatter.9.cloned.1.call-update) | async-done | bytes 524304
  395.8 1.3 copy.95
  397.2 1.0 copy.90
  398.2 1.0 copy.89
  (149 shorter events, 13.0 us)
Async XLA Ops:
  7.2 2.9 copy-start.2
  7.2 3.6 copy-start.25
  7.2 3.6 copy-start.32
  7.2 3.6 copy-start.31
  7.2 3.6 copy-start.30
  7.2 3.6 copy-start.29
  7.2 3.6 copy-start.28
  7.3 3.6 copy-start.27
  7.3 3.8 copy-start.22
  7.3 3.8 copy-start.23
  7.3 123.4 %all-gather.2.cloned.1.call-start = ((), (), s32[]{:S(2)}) async-start(), calls=%async_computation.2 | async-start | bytes 4718592 | tf_op jit(solution)/shard_map/all_gather | solution.py:326
  9.3 221.5 %all-reduce.3.cloned.1.call-start = ((), (), s32[]{:S(2)}) async-start(), calls=%async_computation.3 | async-start | bytes 2097152 | tf_op jit(solution)/shard_map/psum | solution.py:426
  35.5 46.8 %copy-start = (bf16[8,128,1152]{2,1,0:T(8,128)(2,1)}, bf16[8,128,1152]{2,1,0:T(8,128)(2,1)S(1)}, u32[]{:S(2)}) copy-start(bf16[8,128,1152]{2,1,0:T(8,128)(2,1)S(1)} %gather_blocks.2) | copy-start | bytes 7077892
  39.6 1.0 copy-start.18
  39.6 1.8 copy-start.24
  67.6 4.6 %copy-start.26 = (s32[2]{0:T(128)S(1)}, s32[2]{0:T(128)}, u32[]{:S(2)}) copy-start(s32[2]{0:T(128)} %param.16) | copy-start | bytes 28
  72.7 6.3 %copy-start.8 = (pred[2,256,1024]{2,1,0:T(8,128)(4,1)}, pred[2,256,1024]{2,1,0:T(8,128)(4,1)S(1)}, u32[]{:S(2)}) copy-start(pred[2,256,1024]{2,1,0:T(8,128)(4,1)S(1)} %broadcast_and_fusion) | copy-start | bytes 1572868
  75.9 3.2 copy-start.4
  75.9 3.2 copy-start.19
  81.9 0.7 copy-start.21
  82.3 45.7 %copy-start.11 = (bf16[32,8,2,256]{3,1,2,0:T(8,128)(2,1)}, bf16[32,8,2,256]{3,1,2,0:T(8,128)(2,1)S(1)}, u32[]{:S(2)}) copy-start(bf16[32,8,2,256]{3,1,2,0:T(8,128)(2,1)S(1)} %copy.104) | copy-start | bytes 786436
  127.6 1.2 copy-start.7
  130.6 3.3 copy-start.15
  130.7 4.6 %copy-start.33 = (bf16[1024,2048]{1,0:T(8,128)(2,1)S(1)}, bf16[1024,2048]{1,0:T(8,128)(2,1)}, u32[]{:S(2)}) copy-start(bf16[1024,2048]{1,0:T(8,128)(2,1)} %all-gather.2.cloned.1.call-done) | copy-start | bytes 12582916
  133.9 1.3 copy-start.35
  137.8 234.2 %reduce-scatter.7.cloned.1.call-start = ((), (), s32[]{:S(2)}) async-start(), calls=%async_computation.4 | async-start | bytes 2359296
  137.8 6.0 %copy-start.34 = (bf16[1024,2048]{1,0:T(8,128)(2,1)S(1)}, bf16[1024,2048]{1,0:T(8,128)(2,1)}, u32[]{:S(2)}) copy-start(bf16[1024,2048]{1,0:T(8,128)(2,1)} %all-gather.2.cloned.1.call-done) | copy-start | bytes 12582916
  142.8 1.0 copy-start.37
  230.8 4.1 %copy-start.12 = (bf16[32,8,2,256]{3,1,2,0:T(8,128)(2,1)S(1)}, bf16[32,8,2,256]{3,1,2,0:T(8,128)(2,1)}, u32[]{:S(2)}) copy-start(bf16[32,8,2,256]{3,1,2,0:T(8,128)(2,1)} %copy-done.11) | copy-start | bytes 786436
  234.9 1.6 copy-start.5
  234.9 2.6 copy-start.1
  237.5 4.5 %copy-start.9 = (pred[2,256,1024]{2,1,0:T(8,128)(4,1)S(1)}, pred[2,256,1024]{2,1,0:T(8,128)(4,1)}, u32[]{:S(2)}) copy-start(pred[2,256,1024]{2,1,0:T(8,128)(4,1)} %copy-done.8) | copy-start | bytes 1572868
  242.0 6.5 %copy-start.10 = (pred[2,256,1024]{2,1,0:T(8,128)(4,1)S(1)}, pred[2,256,1024]{2,1,0:T(8,128)(4,1)}, u32[]{:S(2)}) copy-start(pred[2,256,1024]{2,1,0:T(8,128)(4,1)} %copy-done.8) | copy-start | bytes 1572868
  242.0 6.5 %copy-start.17 = (bf16[2,256,4,64]{1,3,2,0:T(8,128)(2,1)S(1)}, bf16[2,256,4,64]{1,3,2,0:T(8,128)(2,1)}, u32[]{:S(2)}) copy-start(bf16[2,256,4,64]{1,3,2,0:T(8,128)(2,1)} %copy.79) | copy-start | bytes 786436
  242.0 6.5 %copy-start.20 = (bf16[2,1024,256]{1,2,0:T(8,128)(2,1)S(1)}, bf16[2,1024,256]{1,2,0:T(8,128)(2,1)}, u32[]{:S(2)}) copy-start(bf16[2,1024,256]{1,2,0:T(8,128)(2,1)} %copy.73) | copy-start | bytes 3145732
  248.5 5.5 %copy-start.6 = (bf16[2,1024,256]{1,2,0:T(8,128)(2,1)S(1)}, bf16[2,1024,256]{1,2,0:T(8,128)(2,1)}, u32[]{:S(2)}) copy-start(bf16[2,1024,256]{1,2,0:T(8,128)(2,1)} %copy.75) | copy-start | bytes 3145732
  254.1 2.2 copy-start.13
  287.8 2.5 copy-start.14
  295.8 100.0 %reduce-scatter.9.cloned.1.call-start = ((), (), s32[]{:S(2)}) async-start(), calls=%async_computation.5 | async-start | bytes 4718592
  296.1 3.0 copy-start.16
  296.1 3.0 copy-start.36
  313.6 45.0 %copy-start.3 = (bf16[2,256,1024]{2,1,0:T(8,128)(2,1)S(1)}, bf16[2,256,1024]{2,1,0:T(8,128)(2,1)}, u32[]{:S(2)}) copy-start(bf16[2,256,1024]{2,1,0:T(8,128)(2,1)} %param.15) | copy-start | bytes 3145732
Sparse Core Ops, SparseCore 0:
  10.6 46.9 all-gather.1
  137.9 92.8 all-reduce.2
  295.9 42.6 reduce-scatter.6
  341.8 53.9 reduce-scatter.8
